TPU v7x, 32 devices: a whole 2x2x4 slice. The times are simulated.
32 devices in a mesh: groups: 2 (over x), tm: 8 (over z, y), chan: 2 (over core).
Axes of the slice: x: 2, y: 2, z: 4, core: 2. Of those that a mesh axis runs over, the one named last changes fastest.
Arguments:
- record: bfloat16 [4096, 1024], P(('groups', 'tm'), 'chan'), parts along dimension 0, may hold values from -6 to 6
- pca_map: bfloat16 [1024, 128], P('chan'), may hold values from -0.1875 to 0.1875
- offsets: int32 [16], P(('groups', 'tm')), parts along dimension 0, may hold values from -192 to 192
- exclusion: int32 [2], P('groups'), parts along dimension 0, may hold values from 32 to 128
Outputs:
- profile: float32 [4096], P(('groups', 'tm')), parts along dimension 0
There are 2 independent parts, one for each index of `groups`. A program takes and returns all parts, laid end to end along the dimension named above; an argument that names none is the same for every part. Nothing has to cross between parts.
All inputs are finite; a program needn't handle non-finite values.
Results may differ from a plain program's by a relative error of at most 0.0018.
Values may be sent and summed in bfloat16 or wider, within the bound.
No kernel may reach another device: no remote copies, remote signals or barrier semaphores. Data moves between devices by JAX's collectives and lax.ppermute only.
A program may use at most 128 MiB of HBM per device.

v0:
```python
import jax
import jax.numpy as jnp
from jax import lax
from jax.sharding import PartitionSpec as P

DP = 128
M = 256


def shifted(value, axis, steps):
    count = lax.axis_size(axis)
    pairs = [(source, (source + steps) % count) for source in range(count)]
    return lax.ppermute(value, axis, pairs)


def normalize(segment, rows):
    values = segment.astype(jnp.float32)
    row_pos = lax.broadcasted_iota(jnp.int32, (rows, rows + M - 1), 0)
    col_pos = lax.broadcasted_iota(jnp.int32, (rows, rows + M - 1), 1)
    window = ((col_pos - row_pos >= 0) & (col_pos - row_pos < M)).astype(jnp.float32)
    sums = jnp.dot(window, values, precision=lax.Precision.HIGHEST)
    squares = jnp.dot(window, values * values, precision=lax.Precision.HIGHEST)
    center = sums / M
    spread = squares / M - center * center
    scale = jnp.sqrt(spread + 1e-05) * float(M * DP) ** 0.25
    stacked = jnp.stack([segment[offset : offset + rows] for offset in range(M)], axis=1)
    normed = ((stacked.astype(jnp.float32) - center[:, None, :]) / scale[:, None, :]).astype(
        jnp.bfloat16
    )
    return normed.reshape(rows, M * segment.shape[1])


def tile_product(left, right):
    return lax.dot_general(
        left, right, (((1,), (1,)), ((), ())), preferred_element_type=jnp.float32
    )


def keyed_tile(query_z, segment, rows):
    key_block = min(rows, 128)
    pieces = []
    for first in range(0, rows, key_block):
        keys_z = normalize(segment[first : first + key_block + M - 1], key_block)
        pieces.append(tile_product(query_z, keys_z))
    return jnp.concatenate(pieces, axis=1)


def per_device(record, pca_map, offsets, exclusion):
    cores = lax.axis_size("chan")
    core = lax.axis_index("chan")
    cycle = lax.axis_size("tm")
    rows = record.shape[0]
    share = rows // cores
    start = core * share
    partial_value = jnp.dot(record, pca_map, preferred_element_type=jnp.float32)
    proj = lax.psum(partial_value, "chan").astype(jnp.bfloat16)
    tail = shifted(proj[: M - 1], "tm", -1)
    own_seg = jnp.concatenate([proj, tail], axis=0)
    near_seg = shifted(own_seg, "tm", -1)
    far_seg = shifted(own_seg, "tm", cycle // 2)
    query_seg = lax.dynamic_slice_in_dim(own_seg, start, share + M - 1, 0)
    query_z = normalize(query_seg, share)
    near = keyed_tile(query_z, near_seg, rows)
    other_tile = keyed_tile(query_z, far_seg, rows)
    quarter = rows // 4
    row_pos = start + lax.broadcasted_iota(jnp.int32, (share, rows), 0)
    col_pos = lax.broadcasted_iota(jnp.int32, (share, rows), 1)
    diff = col_pos - row_pos
    centre = offsets[0]
    keep = (diff >= centre - quarter) & (diff <= centre + quarter) & (rows + diff >= exclusion[0])
    near = jnp.where(keep, near, jnp.float32(-1e30))
    empty_rows = jnp.full((rows,), -1e30, jnp.float32)
    row_best = jnp.maximum(jnp.max(near, axis=1), jnp.max(other_tile, axis=1))
    full_rows = lax.dynamic_update_slice_in_dim(empty_rows, row_best, start, 0)
    col_part = jnp.max(near, axis=0)
    col_back = shifted(col_part, "tm", 1)
    row_all, col_all = lax.pmax((full_rows, col_back), "chan")
    return jnp.maximum(row_all, col_all)


def solution(mesh):
    in_specs = (P(("groups", "tm"), "chan"), P("chan", None), P(("groups", "tm")), P("groups"))
    out_specs = P(("groups", "tm"))
    return jax.shard_map(
        per_device, mesh=mesh, in_specs=in_specs, out_specs=out_specs, check_vma=False
    )
```

profile of v0, /device:TPU:0, one launch (start us, length us, event | category | flops | bytes accessed | tf_op | source)
XLA Modules:
  0.0 843.6 jit_solution(11557198780300402680)
XLA Ops:
  0.0 0.9 copy-done
  1.0 1.1 fusion.96
  2.1 4.1 all-reduce.1
  6.2 5.8 collective-permute-start
  15.5 4.7 collective-permute-start.1
  20.2 0.6 constant_dynamic-update-slice_fusion.254
  44.7 0.6 constant_dynamic-update-slice_fusion.214
  46.6 0.6 constant_dynamic-update-slice_fusion.211
  55.1 0.6 constant_dynamic-update-slice_fusion.197
  70.5 0.6 constant_dynamic-update-slice_fusion.172
  72.3 0.6 constant_dynamic-update-slice_fusion.169
  96.8 0.6 constant_dynamic-update-slice_fusion.129
  116.4 0.6 constant_dynamic-update-slice_fusion.97
  118.9 0.6 constant_dynamic-update-slice_fusion.93
  140.3 0.6 constant_dynamic-update-slice_fusion.58
  155.0 0.6 constant_dynamic-update-slice_fusion.34
  169.7 0.6 constant_dynamic-update-slice_fusion.10
  176.8 10.6 %divide_convert_fusion.4 = bf16[128,256,128]{2,0,1:T(8,128)(2,1)} fusion(bf16[128,256,128]{2,0,1:T(8,128)(2,1)} %constant_dynamic-update-slice_fusion, f32[128,128]{1,0:T(8,128)S(1)} %fusion.44, f32[128,128]{1,0:T(8,128)S(1)} %convolution_multiply_fusion.9), kind=kLoop, calls=%fused_computation.4 | loop fusion | flops 16777216 | bytes 16908288 | tf_op jit(solution)/shard_map/convert_element_type | solution.py:27
  194.3 0.6 constant_dynamic-update-slice_fusion.501
  206.6 0.6 constant_dynamic-update-slice_fusion.481
  209.0 0.6 constant_dynamic-update-slice_fusion.477
  240.9 0.6 constant_dynamic-update-slice_fusion.425
  267.2 0.6 constant_dynamic-update-slice_fusion.382
  291.7 0.6 constant_dynamic-update-slice_fusion.342
  293.5 0.6 constant_dynamic-update-slice_fusion.339
  343.8 0.6 constant_dynamic-update-slice_fusion.257
  344.4 0.6 constant_dynamic-update-slice_fusion.766
  345.6 0.8 constant_dynamic-update-slice_fusion.764
  369.0 0.6 constant_dynamic-update-slice_fusion.726
  370.9 0.6 constant_dynamic-update-slice_fusion.723
  379.5 0.6 constant_dynamic-update-slice_fusion.709
  394.8 0.6 constant_dynamic-update-slice_fusion.684
  396.6 0.6 constant_dynamic-update-slice_fusion.681
  421.1 0.6 constant_dynamic-update-slice_fusion.641
  440.7 0.6 constant_dynamic-update-slice_fusion.609
  443.2 0.6 constant_dynamic-update-slice_fusion.605
  464.6 0.6 constant_dynamic-update-slice_fusion.570
  479.4 0.6 constant_dynamic-update-slice_fusion.546
  494.0 0.6 constant_dynamic-update-slice_fusion.522
  500.5 0.6 constant_dynamic-update-slice_fusion.256
  501.1 6.0 fusion.7
  507.6 6.0 fusion.6
  515.4 0.6 constant_dynamic-update-slice_fusion.1278
  539.9 0.6 constant_dynamic-update-slice_fusion.1238
  541.7 0.6 constant_dynamic-update-slice_fusion.1235
  550.3 0.6 constant_dynamic-update-slice_fusion.1221
  565.6 0.6 constant_dynamic-update-slice_fusion.1196
  567.5 0.6 constant_dynamic-update-slice_fusion.1193
  591.9 0.6 constant_dynamic-update-slice_fusion.1153
  611.6 0.6 constant_dynamic-update-slice_fusion.1121
  635.5 0.6 constant_dynamic-update-slice_fusion.1082
  664.9 0.6 constant_dynamic-update-slice_fusion.1034
  688.8 0.6 constant_dynamic-update-slice_fusion.993
  723.1 0.6 constant_dynamic-update-slice_fusion.937
  727.4 0.6 constant_dynamic-update-slice_fusion.930
  742.1 0.6 constant_dynamic-update-slice_fusion.906
  749.5 0.6 constant_dynamic-update-slice_fusion.894
  773.9 0.6 constant_dynamic-update-slice_fusion.854
  799.7 0.6 constant_dynamic-update-slice_fusion.812
  826.0 0.6 constant_dynamic-update-slice_fusion.769
  826.9 0.6 constant_dynamic-update-slice_fusion.768
  827.6 5.9 fusion.24
  834.2 5.8 fusion.25
  840.1 3.0 pmax.16
  (1254 shorter events, 753.4 us)
Async XLA Ops:
  0.0 1.0 copy-start
  6.2 7.7 collective-permute-start
  15.0 499.0 %collective-permute-start.2 = (bf16[511,128]{1,0:T(8,128)(2,1)S(1)}, bf16[511,128]{1,0:T(8,128)(2,1)S(1)}, u32[]{:S(2)}, u32[]{:S(2)}) collective-permute-start(bf16[511,128]{1,0:T(8,128)(2,1)S(1)} %pad_maximum_fusion), channel_id=1, source_target_pairs={{0,8},{2,10},{4,12},{6,14},{8,0},{10,2},{12,4},{14,6},{1,9},{3,11}... | collective-permute-start | bytes 392456 | tf_op jit(solution)/shard_map/ppermute | solution.py:13
  15.5 171.9 %collective-permute-start.1 = (bf16[511,128]{1,0:T(8,128)(2,1)S(1)}, bf16[511,128]{1,0:T(8,128)(2,1)S(1)}, u32[]{:S(2)}, u32[]{:S(2)}) collective-permute-start(bf16[511,128]{1,0:T(8,128)(2,1)S(1)} %pad_maximum_fusion), channel_id=1, source_target_pairs={{0,14},{2,0},{4,2},{6,4},{8,6},{10,8},{12,10},{14,12},{1,15},{3,1}... | collective-permute-start | bytes 392456 | tf_op jit(solution)/shard_map/ppermute | solution.py:13
  348.9 152.2 %slice-start = ((s8[8388608]{0:T(1024)(128)(4,1)}), s8[4194304]{0:T(1024)(128)(4,1)S(1)}, s32[]{:S(2)}) async-start(s8[8388608]{0:T(1024)(128)(4,1)} %bitcast.4632), calls=%async_computation | async-start | bytes 8388608
  426.6 74.5 %slice-start.1 = ((s8[8388608]{0:T(1024)(128)(4,1)}), s8[4194304]{0:T(1024)(128)(4,1)S(1)}, s32[]{:S(2)}) async-start(s8[8388608]{0:T(1024)(128)(4,1)} %bitcast.4632), calls=%async_computation.1 | async-start | bytes 8388608
  513.7 326.4 %collective-permute-start.3 = (f32[256]{0:T(256)S(1)}, f32[256]{0:T(256)S(1)}, u32[]{:S(2)}, u32[]{:S(2)}) collective-permute-start(f32[256]{0:T(256)S(1)} %get-tuple-element.5), channel_id=1, source_target_pairs={{0,2},{2,4},{4,6},{6,8},{8,10},{10,12},{12,14},{14,0},{1,3},{3,5},... | collective-permute-start | bytes 3080 | tf_op jit(solution)/shard_map/ppermute | solution.py:13
where the time goes:
time: 853 us; the launch traced here: 844 us
  local copies, waits for them, and re-layouts  783 us (92%)
  matrix products  27.1 us (3%)
  starting transfers between devices  11.3 us (1%)
  other arithmetic  11.2 us (1%)
    unnamed x1281, local copies, waits for them, and re-layouts  782 us
    dot_general x4, matrix products, tile_product(): lax.dot_general(left, right, (((1,), (1,)), ((), ())), preferred_element_...  23.7 us
  transfers between devices with their start and end apart: 4, of which 1 were waited for; matrix products, arithmetic and copies ran while one was open for 97% of the time, Pallas kernels for 0%

commit v1 on v0

v1 whole, which is shorter than its diff:
```python
import jax
import jax.numpy as jnp
from jax import lax
from jax.experimental import pallas as pl
from jax.experimental.pallas import tpu as pltpu
from jax.sharding import PartitionSpec as P

M = 256
SHIFTS = 16
GROUP = 4
NEG = -1e30


def window_stats(values, rows, scale):
    span = values.shape[0]
    row_pos = lax.broadcasted_iota(jnp.int32, (rows, span), 0)
    col_pos = lax.broadcasted_iota(jnp.int32, (rows, span), 1)
    inside = (col_pos >= row_pos) & (col_pos < row_pos + M)
    band = jnp.where(inside, 1.0, 0.0).astype(jnp.bfloat16)
    square = values * values
    upper = square.astype(jnp.bfloat16)
    lower = (square - upper.astype(jnp.float32)).astype(jnp.bfloat16)
    sums = jnp.dot(band, values.astype(jnp.bfloat16), preferred_element_type=jnp.float32)
    squares = jnp.dot(band, upper, preferred_element_type=jnp.float32)
    squares += jnp.dot(band, lower, preferred_element_type=jnp.float32)
    center = sums / M
    spread = squares / M - center * center
    return center, 1.0 / (jnp.sqrt(spread + 1e-05) * scale)


def tile_kernel(limits, q_head, q_tail, k_head, k_tail, best, wide, shifted, center, inverse, total):
    rows, depth = q_head.shape
    reach = shifted.shape[2]
    scale = float(M * depth) ** 0.25
    for side, (head, tail) in enumerate(((q_head, q_tail), (k_head, k_tail))):
        wide[0:rows, :] = head[...].astype(jnp.float32)
        wide[rows : rows + M, :] = tail[...].astype(jnp.float32)
        center[side], inverse[side] = window_stats(wide[...], rows, scale)
        for shift in range(SHIFTS):
            shifted[side, shift] = wide[shift : shift + reach, :].astype(jnp.bfloat16)
    total[...] = jnp.zeros_like(total)

    def normed(side, shift, base):
        window = shifted[side, shift, pl.ds(base, rows), :].astype(jnp.float32)
        return ((window - center[side]) * inverse[side]).astype(jnp.bfloat16)

    def step(index, carry):
        base = pl.multiple_of(index * SHIFTS, SHIFTS)
        added = jnp.zeros_like(total)
        for first in range(0, SHIFTS, GROUP):
            shifts = range(first, first + GROUP)
            left = jnp.concatenate([normed(0, shift, base) for shift in shifts], axis=1)
            right = jnp.concatenate([normed(1, shift, base) for shift in shifts], axis=1)
            added += lax.dot_general(
                left, right, (((1,), (1,)), ((), ())), preferred_element_type=jnp.float32
            )
        total[...] += added
        return carry

    lax.fori_loop(0, M // SHIFTS, step, 0)
    row_pos = lax.broadcasted_iota(jnp.int32, (rows, rows), 0)
    col_pos = lax.broadcasted_iota(jnp.int32, (rows, rows), 1)
    diff = col_pos - row_pos
    keep = (diff >= limits[0]) & (diff <= limits[1]) & (rows + diff >= limits[2])
    score = jnp.where(keep, total[...], NEG)
    row_best = jnp.max(score, axis=1, keepdims=True)
    best[0:1, :] = jnp.max(jnp.where(diff == 0, row_best, NEG), axis=0, keepdims=True)
    best[1:2, :] = jnp.max(score, axis=0, keepdims=True)


def tile_best(limits, q_head, q_tail, k_head, k_tail):
    rows, depth = q_head.shape
    vmem = pl.BlockSpec(memory_space=pltpu.VMEM)
    reach = rows + M - SHIFTS
    return pl.pallas_call(
        tile_kernel,
        out_shape=jax.ShapeDtypeStruct((2, rows), jnp.float32),
        in_specs=[pl.BlockSpec(memory_space=pltpu.SMEM), vmem, vmem, vmem, vmem],
        out_specs=vmem,
        scratch_shapes=[
            pltpu.VMEM((rows + M, depth), jnp.float32),
            pltpu.VMEM((2, SHIFTS, reach, depth), jnp.bfloat16),
            pltpu.VMEM((2, rows, depth), jnp.float32),
            pltpu.VMEM((2, rows, depth), jnp.float32),
            pltpu.VMEM((rows, rows), jnp.float32),
        ],
        compiler_params=pltpu.CompilerParams(vmem_limit_bytes=32 << 20),
        name="tile_best",
    )(limits, q_head, q_tail, k_head, k_tail)


def fetched(value, near_steps, far_steps):
    cycle = lax.axis_size("tm")
    pairs = []
    for slab in range(cycle):
        for core, steps in ((0, near_steps), (1, far_steps)):
            pairs.append(((slab + steps) % cycle * 2 + core, slab * 2 + core))
    return lax.ppermute(value, ("tm", "chan"), pairs)


def swapped(value):
    return lax.ppermute(value, "chan", [(0, 1), (1, 0)])


def per_device(record, pca_map, offsets, exclusion):
    core = lax.axis_index("chan")
    cycle = lax.axis_size("tm")
    rows = record.shape[0]
    quarter = rows // 4
    partial_value = jnp.dot(record, pca_map, preferred_element_type=jnp.float32)
    proj = (partial_value + swapped(partial_value)).astype(jnp.bfloat16)
    k_head = fetched(proj, 1, cycle // 2)
    k_tail = fetched(proj, 2, cycle // 2 + 1)
    q_tail = jnp.where(core == 0, k_head, swapped(k_head))
    centre = offsets[0]
    near = jnp.stack([centre - quarter, centre + quarter, exclusion[0]])
    far = jnp.array([-2 * rows, 2 * rows, -2 * rows], jnp.int32)
    best = tile_best(jnp.where(core == 0, near, far), proj, q_tail, k_head, k_tail)
    row_best = best[0]
    col_best = jnp.where(core == 0, best[1], NEG)
    col_back = lax.ppermute(col_best, "tm", [(slab, (slab + 1) % cycle) for slab in range(cycle)])
    own = jnp.maximum(row_best, col_back)
    return jnp.maximum(own, swapped(own))


def solution(mesh):
    in_specs = (P(("groups", "tm"), "chan"), P("chan", None), P(("groups", "tm")), P("groups"))
    out_specs = P(("groups", "tm"))
    return jax.shard_map(
        per_device, mesh=mesh, in_specs=in_specs, out_specs=out_specs, check_vma=False
    )
```

time: 853 us -> 38.1 us (0.04); the launches traced: 844 us -> 37.9 us
  local copies, waits for them, and re-layouts: 783 us -> 1 us
  matrix products: 27.1 us -> 1.11 us
  Pallas kernels: 0 us -> 11.9 us
  other arithmetic: 11.2 us -> 0.68 us
  waiting for transfers between devices: 0.6 us -> 10.3 us
    unnamed x1281 -> x4, local copies, waits for them, and re-layouts: 782 us -> 1 us
    dot_general x14 -> x0, matrix products: 26 us -> none  [the longest x4 23.7 us: tile_product(): lax.dot_general(left, right, (((1,), (1,)), ((), ())), preferred_element_...]
    pallas_call x0 -> x1, Pallas kernels: none -> 11.9 us  [tile_best(): pl.pallas_call(tile_kernel, out_shape=jax.ShapeDtypeStruct((2, rows), jnp...]
    convert_element_type x1, other arithmetic: 10.6 us -> 0.02 us  [per_device(): proj = (partial_value + swapped(partial_value)).astype(jnp.bfloat16)]
    ppermute x4 -> x6, waiting for transfers between devices: 0.6 us -> 10.3 us  [the longest x1 5.15 us: per_device(): lax.ppermute(col_best, 'tm', [(slab, (slab + 1) % cycle) for slab in rang...]
  transfers between devices with their start and end apart: 4 -> 6, of which waited for: 1 -> 5; matrix products, arithmetic and copies ran while one was open for 97% -> 0% of each run, Pallas kernels for 0% -> 0%
where the time goes in v1:
time: 38.1 us; the launch traced here: 37.9 us
  Pallas kernels  11.9 us (31%)
  starting transfers between devices  11.6 us (30%)
  waiting for transfers between devices  10.3 us (27%)
  between operations  1.34 us (4%)
  matrix products  1.11 us (3%)
  local copies, waits for them, and re-layouts  1 us (3%)
  other arithmetic  0.68 us (2%)
    pallas_call x1, Pallas kernels, tile_best(): pl.pallas_call(tile_kernel, out_shape=jax.ShapeDtypeStruct((2, rows), jnp...  11.9 us
    ppermute x2, starting transfers between devices, fetched(): return lax.ppermute(value, ('tm', 'chan'), pairs)  7.81 us
    ppermute x1, waiting for transfers between devices, per_device(): lax.ppermute(col_best, 'tm', [(slab, (slab + 1) % cycle) for slab in rang...  5.15 us
    ppermute x1, starting transfers between devices, per_device(): lax.ppermute(col_best, 'tm', [(slab, (slab + 1) % cycle) for slab in rang...  3.27 us
    ppermute x2, waiting for transfers between devices, fetched(): return lax.ppermute(value, ('tm', 'chan'), pairs)  3 us
    ppermute x3, waiting for transfers between devices, swapped(): return lax.ppermute(value, 'chan', [(0, 1), (1, 0)])  2.13 us
    dot_general x1, matrix products, per_device(): partial_value = jnp.dot(record, pca_map, preferred_element_type=jnp.float32)  1.11 us
    unnamed x4, local copies, waits for them, and re-layouts  1 us
  transfers between devices with their start and end apart: 6, of which 5 were waited for; matrix products, arithmetic and copies ran while one was open for 0% of the time, Pallas kernels for 0%

profile of v1, /device:TPU:0, one launch (start us, length us, event | category | flops | bytes accessed | tf_op | source)
XLA Modules:
  0.0 37.9 jit_solution(2325735738935152789)
XLA Ops:
  0.0 0.0 copy-start
  0.0 0.9 %copy-done = bf16[256,512]{1,0:T(8,128)(2,1)S(1)} copy-done((bf16[256,512]{1,0:T(8,128)(2,1)S(1)}, bf16[256,512]{1,0:T(8,128)(2,1)}, u32[]{:S(2)}) %copy-start) | copy-done | bytes 262168
  1.0 1.1 %fusion = f32[256,128]{1,0:T(8,128)S(1)} fusion(bf16[256,512]{1,0:T(8,128)(2,1)S(1)} %copy-done, bf16[512,128]{1,0:T(8,128)(2,1)} %param.6), kind=kOutput, calls=%fused_computation.4 | convolution fusion | flops 33554432 | bytes 524288 | tf_op jit(solution)/shard_map/dot_general | solution.py:110
  2.1 0.5 %collective-permute-start = (f32[256,128]{1,0:T(8,128)S(1)}, f32[256,128]{1,0:T(8,128)S(1)}, u32[]{:S(2)}, u32[]{:S(2)}) collective-permute-start(f32[256,128]{1,0:T(8,128)S(1)} %fusion), channel_id=1, source_target_pairs={{0,1},{1,0},{2,3},{3,2},{4,5},{5,4},{6,7},{7,6},{8,9},{9,8},{10,11... | collective-permute-start | bytes 393224 | tf_op jit(solution)/shard_map/ppermute | solution.py:102
  2.6 1.0 %collective-permute-done = f32[256,128]{1,0:T(8,128)S(1)} collective-permute-done((f32[256,128]{1,0:T(8,128)S(1)}, f32[256,128]{1,0:T(8,128)S(1)}, u32[]{:S(2)}, u32[]{:S(2)}) %collective-permute-start) | collective-permute-done | bytes 131104 | tf_op jit(solution)/shard_map/ppermute | solution.py:102
  3.6 6.0 %collective-permute-start.1 = (bf16[256,128]{1,0:T(8,128)(2,1)S(1)}, bf16[256,128]{1,0:T(8,128)(2,1)S(1)}, u32[]{:S(2)}, u32[]{:S(2)}) collective-permute-start(bf16[256,128]{1,0:T(8,128)(2,1)S(1)} %add_convert_fusion.q_head), channel_id=1, source_target_pairs={{2,0},{9,1},{4,2},{11,3},{6,4},{13,5},{8,6},{15,7},{10,8},{1,9},{1... | collective-permute-start | bytes 196616 | tf_op jit(solution)/shard_map/ppermute | solution.py:98
  10.9 0.0 copy-start.1
  10.9 0.6 %collective-permute-done.1.k_head = bf16[256,128]{1,0:T(8,128)(2,1)S(1)} collective-permute-done((bf16[256,128]{1,0:T(8,128)(2,1)S(1)}, bf16[256,128]{1,0:T(8,128)(2,1)S(1)}, u32[]{:S(2)}, u32[]{:S(2)}) %collective-permute-start.1) | collective-permute-done | bytes 65568 | tf_op jit(solution)/shard_map/ppermute | solution.py:98
  11.5 0.0 collective-permute-start.2
  11.5 0.0 copy-done.1
  11.5 0.1 broadcast_select_fusion.2.limits
  11.6 1.8 %collective-permute-start.3 = (bf16[256,128]{1,0:T(8,128)(2,1)S(1)}, bf16[256,128]{1,0:T(8,128)(2,1)S(1)}, u32[]{:S(2)}, u32[]{:S(2)}) collective-permute-start(bf16[256,128]{1,0:T(8,128)(2,1)S(1)} %add_convert_fusion.q_head), channel_id=1, source_target_pairs={{4,0},{11,1},{6,2},{13,3},{8,4},{15,5},{10,6},{1,7},{12,8},{3,9},{... | collective-permute-start | bytes 196616 | tf_op jit(solution)/shard_map/ppermute | solution.py:98
  13.4 0.0 collective-permute-done.2
  13.5 2.4 %collective-permute-done.3.k_tail = bf16[256,128]{1,0:T(8,128)(2,1)S(1)} collective-permute-done((bf16[256,128]{1,0:T(8,128)(2,1)S(1)}, bf16[256,128]{1,0:T(8,128)(2,1)S(1)}, u32[]{:S(2)}, u32[]{:S(2)}) %collective-permute-start.3) | collective-permute-done | bytes 65568 | tf_op jit(solution)/shard_map/ppermute | solution.py:98
  15.9 11.9 %tile_best.1 = f32[2,256]{1,0:T(2,128)S(1)} custom-call(s32[3]{0:T(128)S(1)} %broadcast_select_fusion.2.limits, bf16[256,128]{1,0:T(8,128)(2,1)S(1)} %add_convert_fusion.q_head, bf16[256,128]{1,0:T(8,128)(2,1)S(1)} %broadcast_select_fusion.q_tail, bf16[256,128]{1,0:T(8,128)(2,1)S(1)} %collective-permute-done.1.k_head, ...), custom_call_target="tpu_custom_call" | custom-call | tf_op jit(solution)/shard_map/tile_best/pallas_call | solution.py:75
  27.8 3.3 %collective-permute-start.4 = (f32[256]{0:T(256)S(1)}, f32[256]{0:T(256)S(1)}, u32[]{:S(2)}, u32[]{:S(2)}) collective-permute-start(f32[256]{0:T(256)S(1)} %bitcast.5), channel_id=1, source_target_pairs={{0,2},{2,4},{4,6},{6,8},{8,10},{10,12},{12,14},{14,0},{1,3},{3,5},... | collective-permute-start | bytes 3080 | tf_op jit(solution)/shard_map/ppermute | solution.py:121
  31.1 5.1 %collective-permute-done.4 = f32[256]{0:T(256)S(1)} collective-permute-done((f32[256]{0:T(256)S(1)}, f32[256]{0:T(256)S(1)}, u32[]{:S(2)}, u32[]{:S(2)}) %collective-permute-start.4) | collective-permute-done | bytes 1056 | tf_op jit(solution)/shard_map/ppermute | solution.py:121
  36.2 0.0 collective-permute-start.5
  36.2 1.1 %collective-permute-done.5 = f32[256]{0:T(256)S(1)} collective-permute-done((f32[256]{0:T(256)S(1)}, f32[256]{0:T(256)S(1)}, u32[]{:S(2)}, u32[]{:S(2)}) %collective-permute-start.5) | collective-permute-done | bytes 1056 | tf_op jit(solution)/shard_map/ppermute | solution.py:102
  37.4 0.6 %max.7 = f32[256]{0:T(256)} maximum(f32[256]{0:T(256)S(1)} %max.6, f32[256]{0:T(256)S(1)} %collective-permute-done.5) | non-fusion elementwise | flops 256 | bytes 3072 | tf_op jit(solution)/shard_map/max | solution.py:123
  (4 shorter events, 0.0 us)
Async XLA Ops:
  0.0 1.0 %copy-start = (bf16[256,512]{1,0:T(8,128)(2,1)S(1)}, bf16[256,512]{1,0:T(8,128)(2,1)}, u32[]{:S(2)}) copy-start(bf16[256,512]{1,0:T(8,128)(2,1)} %param.5) | copy-start | bytes 786436
  2.1 1.5 %collective-permute-start = (f32[256,128]{1,0:T(8,128)S(1)}, f32[256,128]{1,0:T(8,128)S(1)}, u32[]{:S(2)}, u32[]{:S(2)}) collective-permute-start(f32[256,128]{1,0:T(8,128)S(1)} %fusion), channel_id=1, source_target_pairs={{0,1},{1,0},{2,3},{3,2},{4,5},{5,4},{6,7},{7,6},{8,9},{9,8},{10,11... | collective-permute-start | bytes 393224 | tf_op jit(solution)/shard_map/ppermute | solution.py:102
  3.6 7.9 %collective-permute-start.1 = (bf16[256,128]{1,0:T(8,128)(2,1)S(1)}, bf16[256,128]{1,0:T(8,128)(2,1)S(1)}, u32[]{:S(2)}, u32[]{:S(2)}) collective-permute-start(bf16[256,128]{1,0:T(8,128)(2,1)S(1)} %add_convert_fusion.q_head), channel_id=1, source_target_pairs={{2,0},{9,1},{4,2},{11,3},{6,4},{13,5},{8,6},{15,7},{10,8},{1,9},{1... | collective-permute-start | bytes 196616 | tf_op jit(solution)/shard_map/ppermute | solution.py:98
  10.9 0.7 %copy-start.1 = (s32[3]{0:T(128)S(1)}, s32[3]{0:T(128)}, u32[]{:S(2)}) copy-start(s32[3]{0:T(128)} %constant.16.clone) | copy-start | bytes 40
  11.5 2.0 %collective-permute-start.2 = (bf16[256,128]{1,0:T(8,128)(2,1)S(1)}, bf16[256,128]{1,0:T(8,128)(2,1)S(1)}, u32[]{:S(2)}, u32[]{:S(2)}) collective-permute-start(bf16[256,128]{1,0:T(8,128)(2,1)S(1)} %collective-permute-done.1.k_head), channel_id=1, source_target_pairs={{0,1},{1,0},{2,3},{3,2},{4,5},{5,4},{6,7},{7,6},{8,9},{9,8},{10,11... | collective-permute-start | bytes 196616 | tf_op jit(solution)/shard_map/ppermute | solution.py:102
  11.6 4.3 %collective-permute-start.3 = (bf16[256,128]{1,0:T(8,128)(2,1)S(1)}, bf16[256,128]{1,0:T(8,128)(2,1)S(1)}, u32[]{:S(2)}, u32[]{:S(2)}) collective-permute-start(bf16[256,128]{1,0:T(8,128)(2,1)S(1)} %add_convert_fusion.q_head), channel_id=1, source_target_pairs={{4,0},{11,1},{6,2},{13,3},{8,4},{15,5},{10,6},{1,7},{12,8},{3,9},{... | collective-permute-start | bytes 196616 | tf_op jit(solution)/shard_map/ppermute | solution.py:98
  27.8 8.4 %collective-permute-start.4 = (f32[256]{0:T(256)S(1)}, f32[256]{0:T(256)S(1)}, u32[]{:S(2)}, u32[]{:S(2)}) collective-permute-start(f32[256]{0:T(256)S(1)} %bitcast.5), channel_id=1, source_target_pairs={{0,2},{2,4},{4,6},{6,8},{8,10},{10,12},{12,14},{14,0},{1,3},{3,5},... | collective-permute-start | bytes 3080 | tf_op jit(solution)/shard_map/ppermute | solution.py:121
  36.2 1.1 %collective-permute-start.5 = (f32[256]{0:T(256)S(1)}, f32[256]{0:T(256)S(1)}, u32[]{:S(2)}, u32[]{:S(2)}) collective-permute-start(f32[256]{0:T(256)S(1)} %max.6), channel_id=1, source_target_pairs={{0,1},{1,0},{2,3},{3,2},{4,5},{5,4},{6,7},{7,6},{8,9},{9,8},{10,11... | collective-permute-start | bytes 3080 | tf_op jit(solution)/shard_map/ppermute | solution.py:102

commit v2 on v1

v2 whole, which is shorter than its diff:
```python
import jax
import jax.numpy as jnp
from jax import lax
from jax.experimental import pallas as pl
from jax.experimental.pallas import tpu as pltpu
from jax.sharding import PartitionSpec as P

M = 256
SHIFTS = 64
BLOCK = 64
NEG = -1e30
UNITS = 2


def in_unit(body, shape, units):
    pl.run_scoped(body, *[pltpu.ACC(unit)(shape, jnp.float32) for unit in units])


def window_stats(sides, wide, center, inverse):
    rows, depth = sides[0][0].shape
    scale = float(M * depth) ** 0.25
    row_pos = lax.broadcasted_iota(jnp.int32, (rows, rows), 0)
    col_pos = lax.broadcasted_iota(jnp.int32, (rows, rows), 1)
    upper = jnp.where(col_pos >= row_pos, 1.0, 0.0).astype(jnp.bfloat16)
    lower = jnp.where(col_pos < row_pos, 1.0, 0.0).astype(jnp.bfloat16)

    def scoped(*totals):
        rest = []
        for side, parts in enumerate(sides):
            for half, band in enumerate((upper, lower)):
                value = parts[half][...]
                exact = value.astype(jnp.float32)
                wide[side, half * rows : (half + 1) * rows, :] = exact
                square = exact * exact
                rounded = square.astype(jnp.bfloat16)
                rest.append((square - rounded.astype(jnp.float32)).astype(jnp.bfloat16))
                both = jnp.concatenate([value, rounded], axis=1)
                pltpu.matmul_push_rhs(both, staging_register=half, mxu_index=side)
                pltpu.matmul_acc_lhs(totals[side], band, load_staged_rhs=half)
        for half, band in enumerate((upper, lower)):
            both = jnp.concatenate([rest[half], rest[2 + half]], axis=1)
            pltpu.matmul_push_rhs(both, staging_register=half, mxu_index=half)
            pltpu.matmul_acc_lhs(totals[2 + half], band, load_staged_rhs=half)
        small = pltpu.matmul_pop(totals[2]) + pltpu.matmul_pop(totals[3])
        for side in range(2):
            sums = pltpu.matmul_pop(totals[side])
            squares = sums[:, depth:] + small[:, side * depth : (side + 1) * depth]
            mean = sums[:, :depth] / M
            spread = squares / M - mean * mean
            center[side] = mean
            inverse[side] = (1.0 / (jnp.sqrt(spread + 1e-05) * scale))

    in_unit(scoped, (rows, 2 * depth), (0, 1, 0, 1))


def tile_kernel(limits, q_head, q_tail, k_head, k_tail, best, wide, center, inverse):
    rows, depth = q_head.shape
    blocks = rows // BLOCK
    window_stats(((q_head, q_tail), (k_head, k_tail)), wide, center, inverse)

    def normed(side, base, shift, first, count):
        here = slice(first, first + count)
        mean, scale = center[side, here], inverse[side, here]
        parts = []
        for step in range(shift, shift + 2 * UNITS):
            window = wide[side, pl.ds(base + first + step, count), :]
            parts.append(((window - mean) * scale).astype(jnp.bfloat16))
        return [jnp.concatenate(parts[2 * unit : 2 * unit + 2], axis=1) for unit in range(UNITS)]

    def scoped(*totals):
        def step(index, carry):
            base = pl.multiple_of(index * SHIFTS, SHIFTS)
            for shift in range(0, SHIFTS, 2 * UNITS):
                staging = shift // (2 * UNITS) % 2
                keys = normed(1, base, shift, 0, rows)
                for unit in range(UNITS):
                    pltpu.matmul_push_rhs(
                        keys[unit], staging_register=staging, mxu_index=unit, transpose=True
                    )
                for block in range(blocks):
                    query = normed(0, base, shift, block * BLOCK, BLOCK)
                    for unit in range(UNITS):
                        pltpu.matmul_acc_lhs(
                            totals[unit * blocks + block],
                            query[unit],
                            load_staged_rhs=staging if block == 0 else None,
                        )
            return carry

        lax.fori_loop(0, M // SHIFTS, step, 0)
        col_best = None
        for block in range(blocks):
            first = block * BLOCK
            row_pos = first + lax.broadcasted_iota(jnp.int32, (BLOCK, rows), 0)
            col_pos = lax.broadcasted_iota(jnp.int32, (BLOCK, rows), 1)
            diff = col_pos - row_pos
            keep = (diff >= limits[0]) & (diff <= limits[1]) & (rows + diff >= limits[2])
            total = pltpu.matmul_pop(totals[block]) + pltpu.matmul_pop(totals[blocks + block])
            score = jnp.where(keep, total, NEG)
            row_best = jnp.where(diff == 0, jnp.max(score, axis=1, keepdims=True), NEG)
            both = [jnp.max(value, axis=0, keepdims=True) for value in (row_best, score)]
            col_best = both if block == 0 else [jnp.maximum(*two) for two in zip(col_best, both)]
        best[0:1, :], best[1:2, :] = col_best

    in_unit(scoped, (BLOCK, rows), [unit for unit in range(UNITS) for _ in range(blocks)])


def tile_best(limits, q_head, q_tail, k_head, k_tail):
    rows, depth = q_head.shape
    vmem = pl.BlockSpec(memory_space=pltpu.VMEM)
    return pl.pallas_call(
        tile_kernel,
        out_shape=jax.ShapeDtypeStruct((2, rows), jnp.float32),
        in_specs=[pl.BlockSpec(memory_space=pltpu.SMEM), vmem, vmem, vmem, vmem],
        out_specs=vmem,
        scratch_shapes=[
            pltpu.VMEM((2, rows + M, depth), jnp.float32),
            pltpu.VMEM((2, rows, depth), jnp.float32),
            pltpu.VMEM((2, rows, depth), jnp.float32),
        ],
        compiler_params=pltpu.CompilerParams(vmem_limit_bytes=16 << 20),
        name="tile_best",
    )(limits, q_head, q_tail, k_head, k_tail)


def fetched(value, near_steps, far_steps):
    cycle = lax.axis_size("tm")
    pairs = []
    for slab in range(cycle):
        for core, steps in ((0, near_steps), (1, far_steps)):
            if steps is not None:
                pairs.append(((slab + steps) % cycle * 2 + core, slab * 2 + core))
    return lax.ppermute(value, ("tm", "chan"), pairs)


def swapped(value):
    return lax.ppermute(value, "chan", [(0, 1), (1, 0)])


def per_device(record, pca_map, offsets, exclusion):
    core = lax.axis_index("chan")
    cycle = lax.axis_size("tm")
    rows = record.shape[0]
    quarter = rows // 4
    partial_value = jnp.dot(record, pca_map, preferred_element_type=jnp.float32)
    proj = (partial_value + swapped(partial_value)).astype(jnp.bfloat16)
    k_head = fetched(proj, 1, cycle // 2)
    k_tail = fetched(proj, 2, cycle // 2 + 1)
    k_head, k_tail = lax.optimization_barrier((k_head, k_tail))
    q_tail = jnp.where(core == 0, k_head, swapped(k_head))
    centre = offsets[0]
    near = jnp.stack([centre - quarter, centre + quarter, exclusion[0]])
    far = jnp.array([-2 * rows, 2 * rows, -2 * rows], jnp.int32)
    best = tile_best(jnp.where(core == 0, near, far), proj, q_tail, k_head, k_tail)
    row_best = best[0]
    col_best = jnp.where(core == 0, best[1], NEG)
    col_back = lax.ppermute(col_best, "tm", [(slab, (slab + 1) % cycle) for slab in range(cycle)])
    own = jnp.maximum(row_best, col_back)
    return jnp.maximum(own, swapped(own))


def solution(mesh):
    in_specs = (P(("groups", "tm"), "chan"), P("chan", None), P(("groups", "tm")), P("groups"))
    out_specs = P(("groups", "tm"))
    return jax.shard_map(
        per_device, mesh=mesh, in_specs=in_specs, out_specs=out_specs, check_vma=False
    )
```

time: 38.1 us -> 30.8 us (0.81)
  Pallas kernels: 11.9 us -> 7 us
  starting transfers between devices: 11.6 us -> 7.28 us
  waiting for transfers between devices: 10.3 us -> 12.3 us
    pallas_call x1, Pallas kernels: 11.9 us -> 7 us  [tile_best(): pl.pallas_call(tile_kernel, out_shape=jax.ShapeDtypeStruct((2, rows), jnp...]
    ppermute x1, starting transfers between devices: 3.27 us -> 0.34 us  [per_device(): lax.ppermute(col_best, 'tm', [(slab, (slab + 1) % cycle) for slab in rang...]
    ppermute x2, starting transfers between devices: 7.81 us -> 6.42 us  [fetched(): return lax.ppermute(value, ('tm', 'chan'), pairs)]
    ppermute x3, waiting for transfers between devices: 2.13 us -> 3.3 us  [swapped(): return lax.ppermute(value, 'chan', [(0, 1), (1, 0)])]
    ppermute x1, waiting for transfers between devices: 5.15 us -> 5.98 us  [per_device(): lax.ppermute(col_best, 'tm', [(slab, (slab + 1) % cycle) for slab in rang...]
  transfers between devices with their start and end apart: 6 -> 6, of which waited for: 5 -> 6; matrix products, arithmetic and copies ran while one was open for 0% -> 0% of each run, Pallas kernels for 0% -> 0%
where the time goes in v2:
time: 30.8 us; the launch traced here: 30.7 us
  waiting for transfers between devices  12.3 us (40%)
  starting transfers between devices  7.28 us (24%)
  Pallas kernels  7 us (23%)
  between operations  1.34 us (4%)
  matrix products  1.11 us (4%)
  local copies, waits for them, and re-layouts  0.96 us (3%)
  other arithmetic  0.68 us (2%)
    pallas_call x1, Pallas kernels, tile_best(): pl.pallas_call(tile_kernel, out_shape=jax.ShapeDtypeStruct((2, rows), jnp...  7 us
    ppermute x2, starting transfers between devices, fetched(): return lax.ppermute(value, ('tm', 'chan'), pairs)  6.42 us
    ppermute x1, waiting for transfers between devices, per_device(): lax.ppermute(col_best, 'tm', [(slab, (slab + 1) % cycle) for slab in rang...  5.98 us
    ppermute x3, waiting for transfers between devices, swapped(): return lax.ppermute(value, 'chan', [(0, 1), (1, 0)])  3.3 us
    ppermute x2, waiting for transfers between devices, fetched(): return lax.ppermute(value, ('tm', 'chan'), pairs)  3.03 us
    dot_general x1, matrix products, per_device(): partial_value = jnp.dot(record, pca_map, preferred_element_type=jnp.float32)  1.11 us
    unnamed x4, local copies, waits for them, and re-layouts  0.96 us
  transfers between devices with their start and end apart: 6, of which 6 were waited for; matrix products, arithmetic and copies ran while one was open for 0% of the time, Pallas kernels for 0%

profile of v2, /device:TPU:0, one launch (start us, length us, event | category | flops | bytes accessed | tf_op | source)
XLA Modules:
  0.0 30.7 jit_solution(11473568095009916355)
XLA Ops:
  0.0 0.0 copy-start
  0.0 0.9 %copy-done = bf16[256,512]{1,0:T(8,128)(2,1)S(1)} copy-done((bf16[256,512]{1,0:T(8,128)(2,1)S(1)}, bf16[256,512]{1,0:T(8,128)(2,1)}, u32[]{:S(2)}) %copy-start) | copy-done | bytes 262168
  1.0 1.1 %fusion = f32[256,128]{1,0:T(8,128)S(1)} fusion(bf16[256,512]{1,0:T(8,128)(2,1)S(1)} %copy-done, bf16[512,128]{1,0:T(8,128)(2,1)} %param.6), kind=kOutput, calls=%fused_computation.4 | convolution fusion | flops 33554432 | bytes 524288 | tf_op jit(solution)/shard_map/dot_general | solution.py:145
  2.1 0.5 %collective-permute-start = (f32[256,128]{1,0:T(8,128)S(1)}, f32[256,128]{1,0:T(8,128)S(1)}, u32[]{:S(2)}, u32[]{:S(2)}) collective-permute-start(f32[256,128]{1,0:T(8,128)S(1)} %fusion), channel_id=1, source_target_pairs={{0,1},{1,0},{2,3},{3,2},{4,5},{5,4},{6,7},{7,6},{8,9},{9,8},{10,11... | collective-permute-start | bytes 393224 | tf_op jit(solution)/shard_map/ppermute | solution.py:137
  2.6 1.0 %collective-permute-done = f32[256,128]{1,0:T(8,128)S(1)} collective-permute-done((f32[256,128]{1,0:T(8,128)S(1)}, f32[256,128]{1,0:T(8,128)S(1)}, u32[]{:S(2)}, u32[]{:S(2)}) %collective-permute-start) | collective-permute-done | bytes 131104 | tf_op jit(solution)/shard_map/ppermute | solution.py:137
  3.6 6.0 %collective-permute-start.1 = (bf16[256,128]{1,0:T(8,128)(2,1)S(1)}, bf16[256,128]{1,0:T(8,128)(2,1)S(1)}, u32[]{:S(2)}, u32[]{:S(2)}) collective-permute-start(bf16[256,128]{1,0:T(8,128)(2,1)S(1)} %add_convert_fusion.q_head), channel_id=1, source_target_pairs={{2,0},{9,1},{4,2},{11,3},{6,4},{13,5},{8,6},{15,7},{10,8},{1,9},{1... | collective-permute-start | bytes 196616 | tf_op jit(solution)/shard_map/ppermute | solution.py:133
  9.6 0.4 %collective-permute-start.2 = (bf16[256,128]{1,0:T(8,128)(2,1)S(1)}, bf16[256,128]{1,0:T(8,128)(2,1)S(1)}, u32[]{:S(2)}, u32[]{:S(2)}) collective-permute-start(bf16[256,128]{1,0:T(8,128)(2,1)S(1)} %add_convert_fusion.q_head), channel_id=1, source_target_pairs={{4,0},{11,1},{6,2},{13,3},{8,4},{15,5},{10,6},{1,7},{12,8},{3,9},{... | collective-permute-start | bytes 196616 | tf_op jit(solution)/shard_map/ppermute | solution.py:133
  11.3 0.0 copy-start.1
  11.3 0.2 collective-permute-done.1.k_head
  11.5 2.8 %collective-permute-done.2.k_tail = bf16[256,128]{1,0:T(8,128)(2,1)S(1)} collective-permute-done((bf16[256,128]{1,0:T(8,128)(2,1)S(1)}, bf16[256,128]{1,0:T(8,128)(2,1)S(1)}, u32[]{:S(2)}, u32[]{:S(2)}) %collective-permute-start.2) | collective-permute-done | bytes 65568 | tf_op jit(solution)/shard_map/ppermute | solution.py:133
  14.4 0.0 collective-permute-start.3
  14.4 0.0 copy-done.1
  14.4 0.1 broadcast_select_fusion.2.limits
  14.4 1.2 %collective-permute-done.3 = bf16[256,128]{1,0:T(8,128)(2,1)S(1)} collective-permute-done((bf16[256,128]{1,0:T(8,128)(2,1)S(1)}, bf16[256,128]{1,0:T(8,128)(2,1)S(1)}, u32[]{:S(2)}, u32[]{:S(2)}) %collective-permute-start.3) | collective-permute-done | bytes 65568 | tf_op jit(solution)/shard_map/ppermute | solution.py:137
  15.6 7.0 %tile_best.1 = f32[2,256]{1,0:T(2,128)S(1)} custom-call(s32[3]{0:T(128)S(1)} %broadcast_select_fusion.2.limits, bf16[256,128]{1,0:T(8,128)(2,1)S(1)} %add_convert_fusion.q_head, bf16[256,128]{1,0:T(8,128)(2,1)S(1)} %broadcast_select_fusion.q_tail, bf16[256,128]{1,0:T(8,128)(2,1)S(1)} %collective-permute-done.1.k_head, ...), custom_call_target="tpu_custom_call" | custom-call | tf_op jit(solution)/shard_map/tile_best/pallas_call | solution.py:111
  22.6 0.3 %collective-permute-start.4 = (f32[256]{0:T(256)S(1)}, f32[256]{0:T(256)S(1)}, u32[]{:S(2)}, u32[]{:S(2)}) collective-permute-start(f32[256]{0:T(256)S(1)} %bitcast.5), channel_id=1, source_target_pairs={{0,2},{2,4},{4,6},{6,8},{8,10},{10,12},{12,14},{14,0},{1,3},{3,5},... | collective-permute-start | bytes 3080 | tf_op jit(solution)/shard_map/ppermute | solution.py:157
  23.0 6.0 %collective-permute-done.4 = f32[256]{0:T(256)S(1)} collective-permute-done((f32[256]{0:T(256)S(1)}, f32[256]{0:T(256)S(1)}, u32[]{:S(2)}, u32[]{:S(2)}) %collective-permute-start.4) | collective-permute-done | bytes 1056 | tf_op jit(solution)/shard_map/ppermute | solution.py:157
  29.0 0.0 collective-permute-start.5
  29.0 1.1 %collective-permute-done.5 = f32[256]{0:T(256)S(1)} collective-permute-done((f32[256]{0:T(256)S(1)}, f32[256]{0:T(256)S(1)}, u32[]{:S(2)}, u32[]{:S(2)}) %collective-permute-start.5) | collective-permute-done | bytes 1056 | tf_op jit(solution)/shard_map/ppermute | solution.py:137
  30.1 0.6 %max.7 = f32[256]{0:T(256)} maximum(f32[256]{0:T(256)S(1)} %max.6, f32[256]{0:T(256)S(1)} %collective-permute-done.5) | non-fusion elementwise | flops 256 | bytes 3072 | tf_op jit(solution)/shard_map/max | solution.py:159
  (4 shorter events, 0.0 us)
Async XLA Ops:
  0.0 1.0 %copy-start = (bf16[256,512]{1,0:T(8,128)(2,1)S(1)}, bf16[256,512]{1,0:T(8,128)(2,1)}, u32[]{:S(2)}) copy-start(bf16[256,512]{1,0:T(8,128)(2,1)} %param.5) | copy-start | bytes 786436
  2.1 1.5 %collective-permute-start = (f32[256,128]{1,0:T(8,128)S(1)}, f32[256,128]{1,0:T(8,128)S(1)}, u32[]{:S(2)}, u32[]{:S(2)}) collective-permute-start(f32[256,128]{1,0:T(8,128)S(1)} %fusion), channel_id=1, source_target_pairs={{0,1},{1,0},{2,3},{3,2},{4,5},{5,4},{6,7},{7,6},{8,9},{9,8},{10,11... | collective-permute-start | bytes 393224 | tf_op jit(solution)/shard_map/ppermute | solution.py:137
  3.6 7.9 %collective-permute-start.1 = (bf16[256,128]{1,0:T(8,128)(2,1)S(1)}, bf16[256,128]{1,0:T(8,128)(2,1)S(1)}, u32[]{:S(2)}, u32[]{:S(2)}) collective-permute-start(bf16[256,128]{1,0:T(8,128)(2,1)S(1)} %add_convert_fusion.q_head), channel_id=1, source_target_pairs={{2,0},{9,1},{4,2},{11,3},{6,4},{13,5},{8,6},{15,7},{10,8},{1,9},{1... | collective-permute-start | bytes 196616 | tf_op jit(solution)/shard_map/ppermute | solution.py:133
  9.6 4.8 %collective-permute-start.2 = (bf16[256,128]{1,0:T(8,128)(2,1)S(1)}, bf16[256,128]{1,0:T(8,128)(2,1)S(1)}, u32[]{:S(2)}, u32[]{:S(2)}) collective-permute-start(bf16[256,128]{1,0:T(8,128)(2,1)S(1)} %add_convert_fusion.q_head), channel_id=1, source_target_pairs={{4,0},{11,1},{6,2},{13,3},{8,4},{15,5},{10,6},{1,7},{12,8},{3,9},{... | collective-permute-start | bytes 196616 | tf_op jit(solution)/shard_map/ppermute | solution.py:133
  11.3 3.1 %copy-start.1 = (s32[3]{0:T(128)S(1)}, s32[3]{0:T(128)}, u32[]{:S(2)}) copy-start(s32[3]{0:T(128)} %constant.16.clone) | copy-start | bytes 40
  14.4 1.3 %collective-permute-start.3 = (bf16[256,128]{1,0:T(8,128)(2,1)S(1)}, bf16[256,128]{1,0:T(8,128)(2,1)S(1)}, u32[]{:S(2)}, u32[]{:S(2)}) collective-permute-start(bf16[256,128]{1,0:T(8,128)(2,1)S(1)} %collective-permute-done.1.k_head), channel_id=1, source_target_pairs={{0,1},{1,0},{2,3},{3,2},{4,5},{5,4},{6,7},{7,6},{8,9},{9,8},{10,11... | collective-permute-start | bytes 196616 | tf_op jit(solution)/shard_map/ppermute | solution.py:137
  22.6 6.3 %collective-permute-start.4 = (f32[256]{0:T(256)S(1)}, f32[256]{0:T(256)S(1)}, u32[]{:S(2)}, u32[]{:S(2)}) collective-permute-start(f32[256]{0:T(256)S(1)} %bitcast.5), channel_id=1, source_target_pairs={{0,2},{2,4},{4,6},{6,8},{8,10},{10,12},{12,14},{14,0},{1,3},{3,5},... | collective-permute-start | bytes 3080 | tf_op jit(solution)/shard_map/ppermute | solution.py:157
  29.0 1.1 %collective-permute-start.5 = (f32[256]{0:T(256)S(1)}, f32[256]{0:T(256)S(1)}, u32[]{:S(2)}, u32[]{:S(2)}) collective-permute-start(f32[256]{0:T(256)S(1)} %max.6), channel_id=1, source_target_pairs={{0,1},{1,0},{2,3},{3,2},{4,5},{5,4},{6,7},{7,6},{8,9},{9,8},{10,11... | collective-permute-start | bytes 3080 | tf_op jit(solution)/shard_map/ppermute | solution.py:137

commit v3 on v2

--- a/solution.py
+++ b/solution.py
@@ -17,7 +17,7 @@
 
 
 def window_stats(sides, wide, center, inverse):
-    rows, depth = sides[0][0].shape
+    rows, depth = sides[1][0].shape
     scale = float(M * depth) ** 0.25
     row_pos = lax.broadcasted_iota(jnp.int32, (rows, rows), 0)
     col_pos = lax.broadcasted_iota(jnp.int32, (rows, rows), 1)
@@ -28,7 +28,7 @@
         rest = []
         for side, parts in enumerate(sides):
             for half, band in enumerate((upper, lower)):
-                value = parts[half][...]
+                value = parts[half][0:rows, :]
                 exact = value.astype(jnp.float32)
                 wide[side, half * rows : (half + 1) * rows, :] = exact
                 square = exact * exact
@@ -53,10 +53,10 @@
     in_unit(scoped, (rows, 2 * depth), (0, 1, 0, 1))
 
 
-def tile_kernel(limits, q_head, q_tail, k_head, k_tail, best, wide, center, inverse):
-    rows, depth = q_head.shape
+def tile_kernel(bounds, r_head, r_tail, c_head, c_tail, best, wide, center, inverse):
+    rows, depth = c_head.shape
     blocks = rows // BLOCK
-    window_stats(((q_head, q_tail), (k_head, k_tail)), wide, center, inverse)
+    window_stats(((r_head, r_tail), (c_head, c_tail)), wide, center, inverse)
 
     def normed(side, base, shift, first, count):
         here = slice(first, first + count)
@@ -88,25 +88,27 @@
             return carry
 
         lax.fori_loop(0, M // SHIFTS, step, 0)
-        col_best = None
+        quarter = rows // 4
+        centre = r_head[rows : rows + 1, 0:1].astype(jnp.float32).astype(jnp.int32)
+        found = None
         for block in range(blocks):
-            first = block * BLOCK
-            row_pos = first + lax.broadcasted_iota(jnp.int32, (BLOCK, rows), 0)
+            row_pos = block * BLOCK + lax.broadcasted_iota(jnp.int32, (BLOCK, rows), 0)
             col_pos = lax.broadcasted_iota(jnp.int32, (BLOCK, rows), 1)
             diff = col_pos - row_pos
-            keep = (diff >= limits[0]) & (diff <= limits[1]) & (rows + diff >= limits[2])
+            away = jnp.abs(diff - centre)
+            keep = (away <= quarter + bounds[0]) & (rows + diff >= bounds[1])
             total = pltpu.matmul_pop(totals[block]) + pltpu.matmul_pop(totals[blocks + block])
             score = jnp.where(keep, total, NEG)
             row_best = jnp.where(diff == 0, jnp.max(score, axis=1, keepdims=True), NEG)
-            both = [jnp.max(value, axis=0, keepdims=True) for value in (row_best, score)]
-            col_best = both if block == 0 else [jnp.maximum(*two) for two in zip(col_best, both)]
-        best[0:1, :], best[1:2, :] = col_best
+            both = [jnp.max(value, axis=0, keepdims=True) for value in (score, row_best)]
+            found = both if found is None else [jnp.maximum(*two) for two in zip(found, both)]
+        best[0:1, :], best[1:2, :] = found
 
     in_unit(scoped, (BLOCK, rows), [unit for unit in range(UNITS) for _ in range(blocks)])
 
 
-def tile_best(limits, q_head, q_tail, k_head, k_tail):
-    rows, depth = q_head.shape
+def tile_best(bounds, r_head, r_tail, c_head, c_tail):
+    rows, depth = c_head.shape
     vmem = pl.BlockSpec(memory_space=pltpu.VMEM)
     return pl.pallas_call(
         tile_kernel,
@@ -120,7 +122,7 @@
         ],
         compiler_params=pltpu.CompilerParams(vmem_limit_bytes=16 << 20),
         name="tile_best",
-    )(limits, q_head, q_tail, k_head, k_tail)
+    )(bounds, r_head, r_tail, c_head, c_tail)
 
 
 def fetched(value, near_steps, far_steps):
@@ -141,21 +143,19 @@
     core = lax.axis_index("chan")
     cycle = lax.axis_size("tm")
     rows = record.shape[0]
-    quarter = rows // 4
     partial_value = jnp.dot(record, pca_map, preferred_element_type=jnp.float32)
     proj = (partial_value + swapped(partial_value)).astype(jnp.bfloat16)
-    k_head = fetched(proj, 1, cycle // 2)
-    k_tail = fetched(proj, 2, cycle // 2 + 1)
-    k_head, k_tail = lax.optimization_barrier((k_head, k_tail))
-    q_tail = jnp.where(core == 0, k_head, swapped(k_head))
-    centre = offsets[0]
-    near = jnp.stack([centre - quarter, centre + quarter, exclusion[0]])
-    far = jnp.array([-2 * rows, 2 * rows, -2 * rows], jnp.int32)
-    best = tile_best(jnp.where(core == 0, near, far), proj, q_tail, k_head, k_tail)
-    row_best = best[0]
-    col_best = jnp.where(core == 0, best[1], NEG)
-    col_back = lax.ppermute(col_best, "tm", [(slab, (slab + 1) % cycle) for slab in range(cycle)])
-    own = jnp.maximum(row_best, col_back)
+    note = jnp.broadcast_to(offsets.astype(jnp.bfloat16)[:, None], (16, proj.shape[1]))
+    noted = jnp.concatenate([proj, note], axis=0)
+    r_head = fetched(noted, -1, cycle // 2)
+    second = fetched(proj, 1, cycle // 2 + 1)
+    r_head, second = lax.optimization_barrier((r_head, second))
+    r_tail = jnp.where(core == 0, proj, second)
+    c_tail = jnp.where(core == 0, second, swapped(second))
+    bounds = jnp.stack([core * 4 * rows, exclusion[0] - core * 4 * rows])
+    best = tile_best(bounds, r_head, r_tail, proj, c_tail)
+    row_back = lax.ppermute(best[1], "tm", [(slab, (slab - 1) % cycle) for slab in range(cycle)])
+    own = jnp.where(core == 0, jnp.maximum(best[0], row_back), best[0])
     return jnp.maximum(own, swapped(own))
 
 

time: 30.8 us -> 28.2 us (0.916)
  waiting for transfers between devices: 12.3 us -> 5.44 us
  starting transfers between devices: 7.28 us -> 11.5 us
    ppermute x1, waiting for transfers between devices: 5.98 us -> 1.3 us  [per_device(): lax.ppermute(best[1], 'tm', [(slab, (slab - 1) % cycle) for slab in range...]
    ppermute x1, starting transfers between devices: 0.34 us -> 4.47 us  [per_device(): lax.ppermute(best[1], 'tm', [(slab, (slab - 1) % cycle) for slab in range...]
    ppermute x2, waiting for transfers between devices: 3.03 us -> 1.84 us  [fetched(): return lax.ppermute(value, ('tm', 'chan'), pairs)]
    ppermute x3, waiting for transfers between devices: 3.3 us -> 2.29 us  [swapped(): return lax.ppermute(value, 'chan', [(0, 1), (1, 0)])]
    ppermute x3, starting transfers between devices: 0.52 us -> 1.03 us  [swapped(): return lax.ppermute(value, 'chan', [(0, 1), (1, 0)])]
    ppermute x2, starting transfers between devices: 6.42 us -> 6.04 us  [fetched(): return lax.ppermute(value, ('tm', 'chan'), pairs)]
    unnamed x4 -> x2, local copies, waits for them, and re-layouts: 0.96 us -> 0.95 us
where the time goes in v3:
time: 28.2 us; the launch traced here: 28 us
  starting transfers between devices  11.5 us (41%)
  Pallas kernels  6.97 us (25%)
  waiting for transfers between devices  5.44 us (19%)
  between operations  1.34 us (5%)
  matrix products  1.11 us (4%)
  local copies, waits for them, and re-layouts  0.96 us (3%)
  other arithmetic  0.67 us (2%)
    pallas_call x1, Pallas kernels, tile_best(): pl.pallas_call(tile_kernel, out_shape=jax.ShapeDtypeStruct((2, rows), jnp...  6.97 us
    ppermute x2, starting transfers between devices, fetched(): return lax.ppermute(value, ('tm', 'chan'), pairs)  6.04 us
    ppermute x1, starting transfers between devices, per_device(): lax.ppermute(best[1], 'tm', [(slab, (slab - 1) % cycle) for slab in range...  4.47 us
    ppermute x3, waiting for transfers between devices, swapped(): return lax.ppermute(value, 'chan', [(0, 1), (1, 0)])  2.29 us
    ppermute x2, waiting for transfers between devices, fetched(): return lax.ppermute(value, ('tm', 'chan'), pairs)  1.84 us
    ppermute x1, waiting for transfers between devices, per_device(): lax.ppermute(best[1], 'tm', [(slab, (slab - 1) % cycle) for slab in range...  1.3 us
    dot_general x1, matrix products, per_device(): partial_value = jnp.dot(record, pca_map, preferred_element_type=jnp.float32)  1.11 us
    ppermute x3, starting transfers between devices, swapped(): return lax.ppermute(value, 'chan', [(0, 1), (1, 0)])  1.03 us
  transfers between devices with their start and end apart: 6, of which 6 were waited for; matrix products, arithmetic and copies ran while one was open for 0% of the time, Pallas kernels for 0%

profile of v3, /device:TPU:0, one launch (start us, length us, event | category | flops | bytes accessed | tf_op | source)
XLA Modules:
  0.0 28.0 jit_solution(6755793418723266461)
XLA Ops:
  0.0 0.0 copy-start
  0.0 0.9 %copy-done = bf16[256,512]{1,0:T(8,128)(2,1)S(1)} copy-done((bf16[256,512]{1,0:T(8,128)(2,1)S(1)}, bf16[256,512]{1,0:T(8,128)(2,1)}, u32[]{:S(2)}) %copy-start) | copy-done | bytes 262168
  1.0 1.1 %fusion.1 = f32[256,128]{1,0:T(8,128)S(1)} fusion(bf16[256,512]{1,0:T(8,128)(2,1)S(1)} %copy-done, bf16[512,128]{1,0:T(8,128)(2,1)} %param.5), kind=kOutput, calls=%fused_computation.6 | convolution fusion | flops 33554432 | bytes 524288 | tf_op jit(solution)/shard_map/dot_general | solution.py:146
  2.1 0.5 %collective-permute-start = (f32[256,128]{1,0:T(8,128)S(1)}, f32[256,128]{1,0:T(8,128)S(1)}, u32[]{:S(2)}, u32[]{:S(2)}) collective-permute-start(f32[256,128]{1,0:T(8,128)S(1)} %fusion.1), channel_id=1, source_target_pairs={{0,1},{1,0},{2,3},{3,2},{4,5},{5,4},{6,7},{7,6},{8,9},{9,8},{10,11... | collective-permute-start | bytes 393224 | tf_op jit(solution)/shard_map/ppermute | solution.py:139
  3.2 0.3 %collective-permute-done = f32[256,128]{1,0:T(8,128)S(1)} collective-permute-done((f32[256,128]{1,0:T(8,128)S(1)}, f32[256,128]{1,0:T(8,128)S(1)}, u32[]{:S(2)}, u32[]{:S(2)}) %collective-permute-start) | collective-permute-done | bytes 131104 | tf_op jit(solution)/shard_map/ppermute | solution.py:139
  3.6 2.9 %collective-permute-start.1 = (bf16[272,128]{1,0:T(8,128)(2,1)S(1)}, bf16[272,128]{1,0:T(8,128)(2,1)S(1)}, u32[]{:S(2)}, u32[]{:S(2)}) collective-permute-start(bf16[272,128]{1,0:T(8,128)(2,1)S(1)} %concatenate.3), channel_id=1, source_target_pairs={{14,0},{9,1},{0,2},{11,3},{2,4},{13,5},{4,6},{15,7},{6,8},{1,9},{8... | collective-permute-start | bytes 208904 | tf_op jit(solution)/shard_map/ppermute | solution.py:135
  6.5 3.1 %collective-permute-start.2 = (bf16[256,128]{1,0:T(8,128)(2,1)S(1)}, bf16[256,128]{1,0:T(8,128)(2,1)S(1)}, u32[]{:S(2)}, u32[]{:S(2)}) collective-permute-start(bf16[256,128]{1,0:T(8,128)(2,1)S(1)} %add_convert_fusion.c_head), channel_id=1, source_target_pairs={{2,0},{11,1},{4,2},{13,3},{6,4},{15,5},{8,6},{1,7},{10,8},{3,9},{1... | collective-permute-start | bytes 196616 | tf_op jit(solution)/shard_map/ppermute | solution.py:135
  10.3 1.3 %collective-permute-done.2 = bf16[256,128]{1,0:T(8,128)(2,1)S(1)} collective-permute-done((bf16[256,128]{1,0:T(8,128)(2,1)S(1)}, bf16[256,128]{1,0:T(8,128)(2,1)S(1)}, u32[]{:S(2)}, u32[]{:S(2)}) %collective-permute-start.2) | collective-permute-done | bytes 65568 | tf_op jit(solution)/shard_map/ppermute | solution.py:135
  11.6 0.6 %collective-permute-done.1.r_head = bf16[272,128]{1,0:T(8,128)(2,1)S(1)} collective-permute-done((bf16[272,128]{1,0:T(8,128)(2,1)S(1)}, bf16[272,128]{1,0:T(8,128)(2,1)S(1)}, u32[]{:S(2)}, u32[]{:S(2)}) %collective-permute-start.1) | collective-permute-done | bytes 69664 | tf_op jit(solution)/shard_map/ppermute | solution.py:135
  12.1 0.5 %collective-permute-start.3 = (bf16[256,128]{1,0:T(8,128)(2,1)S(1)}, bf16[256,128]{1,0:T(8,128)(2,1)S(1)}, u32[]{:S(2)}, u32[]{:S(2)}) collective-permute-start(bf16[256,128]{1,0:T(8,128)(2,1)S(1)} %collective-permute-done.2), channel_id=1, source_target_pairs={{0,1},{1,0},{2,3},{3,2},{4,5},{5,4},{6,7},{7,6},{8,9},{9,8},{10,11... | collective-permute-start | bytes 196616 | tf_op jit(solution)/shard_map/ppermute | solution.py:139
  12.7 0.1 pad_add_fusion.bounds
  12.7 0.8 %collective-permute-done.3 = bf16[256,128]{1,0:T(8,128)(2,1)S(1)} collective-permute-done((bf16[256,128]{1,0:T(8,128)(2,1)S(1)}, bf16[256,128]{1,0:T(8,128)(2,1)S(1)}, u32[]{:S(2)}, u32[]{:S(2)}) %collective-permute-start.3) | collective-permute-done | bytes 65568 | tf_op jit(solution)/shard_map/ppermute | solution.py:139
  13.6 7.0 %tile_best.1 = f32[2,256]{1,0:T(2,128)S(1)} custom-call(s32[2]{0:T(128)S(1)} %pad_add_fusion.bounds, bf16[272,128]{1,0:T(8,128)(2,1)S(1)} %collective-permute-done.1.r_head, bf16[256,128]{1,0:T(8,128)(2,1)S(1)} %get-tuple-element.10.r_tail, bf16[256,128]{1,0:T(8,128)(2,1)S(1)} %add_convert_fusion.c_head, bf16[256,128]{1,0:T(8,128)(2,1)S(1)} %get-tuple-element.9.c_tail), custom_call_target="tpu_custom_call" | custom-call | tf_op jit(solution)/shard_map/tile_best/pallas_call | solution.py:113
  20.6 4.5 %collective-permute-start.4 = (f32[256]{0:T(256)S(1)}, f32[256]{0:T(256)S(1)}, u32[]{:S(2)}, u32[]{:S(2)}) collective-permute-start(f32[256]{0:T(256)S(1)} %bitcast.10), channel_id=1, source_target_pairs={{0,14},{2,0},{4,2},{6,4},{8,6},{10,8},{12,10},{14,12},{1,15},{3,1}... | collective-permute-start | bytes 3080 | tf_op jit(solution)/shard_map/ppermute | solution.py:157
  25.0 1.3 %collective-permute-done.4 = f32[256]{0:T(256)S(1)} collective-permute-done((f32[256]{0:T(256)S(1)}, f32[256]{0:T(256)S(1)}, u32[]{:S(2)}, u32[]{:S(2)}) %collective-permute-start.4) | collective-permute-done | bytes 1056 | tf_op jit(solution)/shard_map/ppermute | solution.py:157
  26.3 0.0 collective-permute-start.5
  26.3 1.1 %collective-permute-done.5 = f32[256]{0:T(256)S(1)} collective-permute-done((f32[256]{0:T(256)S(1)}, f32[256]{0:T(256)S(1)}, u32[]{:S(2)}, u32[]{:S(2)}) %collective-permute-start.5) | collective-permute-done | bytes 1056 | tf_op jit(solution)/shard_map/ppermute | solution.py:139
  27.5 0.6 %max.7 = f32[256]{0:T(256)} maximum(f32[256]{0:T(256)S(1)} %maximum_select_fusion, f32[256]{0:T(256)S(1)} %collective-permute-done.5) | non-fusion elementwise | flops 256 | bytes 3072 | tf_op jit(solution)/shard_map/max | solution.py:159
  (5 shorter events, 0.0 us)
Async XLA Ops:
  0.0 1.0 %copy-start = (bf16[256,512]{1,0:T(8,128)(2,1)S(1)}, bf16[256,512]{1,0:T(8,128)(2,1)}, u32[]{:S(2)}) copy-start(bf16[256,512]{1,0:T(8,128)(2,1)} %param.4) | copy-start | bytes 786436
  2.1 1.5 %collective-permute-start = (f32[256,128]{1,0:T(8,128)S(1)}, f32[256,128]{1,0:T(8,128)S(1)}, u32[]{:S(2)}, u32[]{:S(2)}) collective-permute-start(f32[256,128]{1,0:T(8,128)S(1)} %fusion.1), channel_id=1, source_target_pairs={{0,1},{1,0},{2,3},{3,2},{4,5},{5,4},{6,7},{7,6},{8,9},{9,8},{10,11... | collective-permute-start | bytes 393224 | tf_op jit(solution)/shard_map/ppermute | solution.py:139
  3.6 8.5 %collective-permute-start.1 = (bf16[272,128]{1,0:T(8,128)(2,1)S(1)}, bf16[272,128]{1,0:T(8,128)(2,1)S(1)}, u32[]{:S(2)}, u32[]{:S(2)}) collective-permute-start(bf16[272,128]{1,0:T(8,128)(2,1)S(1)} %concatenate.3), channel_id=1, source_target_pairs={{14,0},{9,1},{0,2},{11,3},{2,4},{13,5},{4,6},{15,7},{6,8},{1,9},{8... | collective-permute-start | bytes 208904 | tf_op jit(solution)/shard_map/ppermute | solution.py:135
  6.5 5.0 %collective-permute-start.2 = (bf16[256,128]{1,0:T(8,128)(2,1)S(1)}, bf16[256,128]{1,0:T(8,128)(2,1)S(1)}, u32[]{:S(2)}, u32[]{:S(2)}) collective-permute-start(bf16[256,128]{1,0:T(8,128)(2,1)S(1)} %add_convert_fusion.c_head), channel_id=1, source_target_pairs={{2,0},{11,1},{4,2},{13,3},{6,4},{15,5},{8,6},{1,7},{10,8},{3,9},{1... | collective-permute-start | bytes 196616 | tf_op jit(solution)/shard_map/ppermute | solution.py:135
  12.1 1.4 %collective-permute-start.3 = (bf16[256,128]{1,0:T(8,128)(2,1)S(1)}, bf16[256,128]{1,0:T(8,128)(2,1)S(1)}, u32[]{:S(2)}, u32[]{:S(2)}) collective-permute-start(bf16[256,128]{1,0:T(8,128)(2,1)S(1)} %collective-permute-done.2), channel_id=1, source_target_pairs={{0,1},{1,0},{2,3},{3,2},{4,5},{5,4},{6,7},{7,6},{8,9},{9,8},{10,11... | collective-permute-start | bytes 196616 | tf_op jit(solution)/shard_map/ppermute | solution.py:139
  20.6 5.8 %collective-permute-start.4 = (f32[256]{0:T(256)S(1)}, f32[256]{0:T(256)S(1)}, u32[]{:S(2)}, u32[]{:S(2)}) collective-permute-start(f32[256]{0:T(256)S(1)} %bitcast.10), channel_id=1, source_target_pairs={{0,14},{2,0},{4,2},{6,4},{8,6},{10,8},{12,10},{14,12},{1,15},{3,1}... | collective-permute-start | bytes 3080 | tf_op jit(solution)/shard_map/ppermute | solution.py:157
  26.3 1.1 %collective-permute-start.5 = (f32[256]{0:T(256)S(1)}, f32[256]{0:T(256)S(1)}, u32[]{:S(2)}, u32[]{:S(2)}) collective-permute-start(f32[256]{0:T(256)S(1)} %maximum_select_fusion), channel_id=1, source_target_pairs={{0,1},{1,0},{2,3},{3,2},{4,5},{5,4},{6,7},{7,6},{8,9},{9,8},{10,11... | collective-permute-start | bytes 3080 | tf_op jit(solution)/shard_map/ppermute | solution.py:139

commit v4 on v3

--- a/solution.py
+++ b/solution.py
@@ -1,3 +1,5 @@
+import functools
+
 import jax
 import jax.numpy as jnp
 from jax import lax
@@ -10,6 +12,7 @@
 BLOCK = 64
 NEG = -1e30
 UNITS = 2
+CHUNKS = 1
 
 
 def in_unit(body, shape, units):
@@ -125,6 +128,42 @@
     )(bounds, r_head, r_tail, c_head, c_tail)
 
 
+def project_kernel(chunk, record, pca_map, partial_sum, samples, weights, arrived):
+    copies = [pltpu.make_async_copy(pca_map, weights, arrived.at[0])]
+    for first in range(0, record.shape[0], chunk):
+        here = pl.ds(first, chunk)
+        sem = arrived.at[1 + first // chunk]
+        copies.append(pltpu.make_async_copy(record.at[here], samples.at[here], sem))
+    for copy in copies:
+        copy.start()
+    copies[0].wait()
+    for first, copy in zip(range(0, record.shape[0], chunk), copies[1:]):
+        copy.wait()
+        here = slice(first, first + chunk)
+        partial_sum[here, :] = jnp.dot(
+            samples[here, :], weights[...], preferred_element_type=jnp.float32
+        )
+
+
+def project(record, pca_map):
+    rows, depth = record.shape[0], pca_map.shape[1]
+    chunk = rows // CHUNKS
+    hbm = pl.BlockSpec(memory_space=pltpu.HBM)
+    return pl.pallas_call(
+        functools.partial(project_kernel, chunk),
+        out_shape=pltpu.VMEM((rows, depth), jnp.float32),
+        in_specs=[hbm, hbm],
+        out_specs=pl.BlockSpec(memory_space=pltpu.VMEM),
+        scratch_shapes=[
+            pltpu.VMEM(record.shape, record.dtype),
+            pltpu.VMEM(pca_map.shape, pca_map.dtype),
+            pltpu.SemaphoreType.DMA((1 + CHUNKS,)),
+        ],
+        compiler_params=pltpu.CompilerParams(vmem_limit_bytes=4 << 20),
+        name="project",
+    )(*(pltpu.with_memory_space_constraint(x, pltpu.HBM) for x in (record, pca_map)))
+
+
 def fetched(value, near_steps, far_steps):
     cycle = lax.axis_size("tm")
     pairs = []
@@ -143,7 +182,7 @@
     core = lax.axis_index("chan")
     cycle = lax.axis_size("tm")
     rows = record.shape[0]
-    partial_value = jnp.dot(record, pca_map, preferred_element_type=jnp.float32)
+    partial_value = project(record, pca_map)
     proj = (partial_value + swapped(partial_value)).astype(jnp.bfloat16)
     note = jnp.broadcast_to(offsets.astype(jnp.bfloat16)[:, None], (16, proj.shape[1]))
     noted = jnp.concatenate([proj, note], axis=0)

time: 28.2 us -> 27.4 us (0.972)
  Pallas kernels: 6.97 us -> 8.23 us
  matrix products: 1.11 us -> 0 us
  local copies, waits for them, and re-layouts: 0.96 us -> 0.01 us
    pallas_call x0 -> x1, Pallas kernels: none -> 1.25 us  [project(): pl.pallas_call(functools.partial(project_kernel, chunk), out_shape=pltpu....]
    dot_general x1 -> x0, matrix products: 1.11 us -> none  [per_device(): partial_value = jnp.dot(record, pca_map, preferred_element_type=jnp.float32)]
    unnamed x2 -> x0, local copies, waits for them, and re-layouts: 0.95 us -> none
where the time goes in v4:
time: 27.4 us; the launch traced here: 27.2 us
  starting transfers between devices  11.5 us (42%)
  Pallas kernels  8.23 us (30%)
  waiting for transfers between devices  5.45 us (20%)
  between operations  1.34 us (5%)
  other arithmetic  0.67 us (2%)
    pallas_call x1, Pallas kernels, tile_best(): pl.pallas_call(tile_kernel, out_shape=jax.ShapeDtypeStruct((2, rows), jnp...  6.98 us
    ppermute x2, starting transfers between devices, fetched(): return lax.ppermute(value, ('tm', 'chan'), pairs)  6.03 us
    ppermute x1, starting transfers between devices, per_device(): lax.ppermute(best[1], 'tm', [(slab, (slab - 1) % cycle) for slab in range...  4.46 us
    ppermute x3, waiting for transfers between devices, swapped(): return lax.ppermute(value, 'chan', [(0, 1), (1, 0)])  2.29 us
    ppermute x2, waiting for transfers between devices, fetched(): return lax.ppermute(value, ('tm', 'chan'), pairs)  1.86 us
    ppermute x1, waiting for transfers between devices, per_device(): lax.ppermute(best[1], 'tm', [(slab, (slab - 1) % cycle) for slab in range...  1.3 us
    pallas_call x1, Pallas kernels, project(): pl.pallas_call(functools.partial(project_kernel, chunk), out_shape=pltpu....  1.25 us
    ppermute x3, starting transfers between devices, swapped(): return lax.ppermute(value, 'chan', [(0, 1), (1, 0)])  1.02 us
  transfers between devices with their start and end apart: 6, of which 6 were waited for; matrix products, arithmetic and copies ran while one was open for 0% of the time, Pallas kernels for 0%

profile of v4, /device:TPU:0, one launch (start us, length us, event | category | flops | bytes accessed | tf_op | source)
XLA Modules:
  0.0 27.2 jit_solution(8568897008005535871)
XLA Ops:
  0.0 1.3 %project.1 = f32[256,128]{1,0:T(8,128)S(1)} custom-call(bf16[256,512]{1,0:T(8,128)(2,1)} %record.1, bf16[512,128]{1,0:T(8,128)(2,1)} %pca_map.1), custom_call_target="tpu_custom_call" | custom-call | tf_op jit(solution)/shard_map/project/pallas_call | solution.py:152
  1.3 0.5 %collective-permute-start = (f32[256,128]{1,0:T(8,128)S(1)}, f32[256,128]{1,0:T(8,128)S(1)}, u32[]{:S(2)}, u32[]{:S(2)}) collective-permute-start(f32[256,128]{1,0:T(8,128)S(1)} %project.1), channel_id=1, source_target_pairs={{0,1},{1,0},{2,3},{3,2},{4,5},{5,4},{6,7},{7,6},{8,9},{9,8},{10,11... | collective-permute-start | bytes 393224 | tf_op jit(solution)/shard_map/ppermute | solution.py:178
  2.4 0.3 %collective-permute-done = f32[256,128]{1,0:T(8,128)S(1)} collective-permute-done((f32[256,128]{1,0:T(8,128)S(1)}, f32[256,128]{1,0:T(8,128)S(1)}, u32[]{:S(2)}, u32[]{:S(2)}) %collective-permute-start) | collective-permute-done | bytes 131104 | tf_op jit(solution)/shard_map/ppermute | solution.py:178
  2.8 2.9 %collective-permute-start.1 = (bf16[272,128]{1,0:T(8,128)(2,1)S(1)}, bf16[272,128]{1,0:T(8,128)(2,1)S(1)}, u32[]{:S(2)}, u32[]{:S(2)}) collective-permute-start(bf16[272,128]{1,0:T(8,128)(2,1)S(1)} %concatenate.3), channel_id=1, source_target_pairs={{14,0},{9,1},{0,2},{11,3},{2,4},{13,5},{4,6},{15,7},{6,8},{1,9},{8... | collective-permute-start | bytes 208904 | tf_op jit(solution)/shard_map/ppermute | solution.py:174
  5.7 3.1 %collective-permute-start.2 = (bf16[256,128]{1,0:T(8,128)(2,1)S(1)}, bf16[256,128]{1,0:T(8,128)(2,1)S(1)}, u32[]{:S(2)}, u32[]{:S(2)}) collective-permute-start(bf16[256,128]{1,0:T(8,128)(2,1)S(1)} %add_convert_fusion.c_head), channel_id=1, source_target_pairs={{2,0},{11,1},{4,2},{13,3},{6,4},{15,5},{8,6},{1,7},{10,8},{3,9},{1... | collective-permute-start | bytes 196616 | tf_op jit(solution)/shard_map/ppermute | solution.py:174
  9.5 1.3 %collective-permute-done.2 = bf16[256,128]{1,0:T(8,128)(2,1)S(1)} collective-permute-done((bf16[256,128]{1,0:T(8,128)(2,1)S(1)}, bf16[256,128]{1,0:T(8,128)(2,1)S(1)}, u32[]{:S(2)}, u32[]{:S(2)}) %collective-permute-start.2) | collective-permute-done | bytes 65568 | tf_op jit(solution)/shard_map/ppermute | solution.py:174
  10.7 0.6 %collective-permute-done.1.r_head = bf16[272,128]{1,0:T(8,128)(2,1)S(1)} collective-permute-done((bf16[272,128]{1,0:T(8,128)(2,1)S(1)}, bf16[272,128]{1,0:T(8,128)(2,1)S(1)}, u32[]{:S(2)}, u32[]{:S(2)}) %collective-permute-start.1) | collective-permute-done | bytes 69664 | tf_op jit(solution)/shard_map/ppermute | solution.py:174
  11.3 0.5 %collective-permute-start.3 = (bf16[256,128]{1,0:T(8,128)(2,1)S(1)}, bf16[256,128]{1,0:T(8,128)(2,1)S(1)}, u32[]{:S(2)}, u32[]{:S(2)}) collective-permute-start(bf16[256,128]{1,0:T(8,128)(2,1)S(1)} %collective-permute-done.2), channel_id=1, source_target_pairs={{0,1},{1,0},{2,3},{3,2},{4,5},{5,4},{6,7},{7,6},{8,9},{9,8},{10,11... | collective-permute-start | bytes 196616 | tf_op jit(solution)/shard_map/ppermute | solution.py:178
  11.8 0.1 pad_add_fusion.bounds
  11.9 0.8 %collective-permute-done.3 = bf16[256,128]{1,0:T(8,128)(2,1)S(1)} collective-permute-done((bf16[256,128]{1,0:T(8,128)(2,1)S(1)}, bf16[256,128]{1,0:T(8,128)(2,1)S(1)}, u32[]{:S(2)}, u32[]{:S(2)}) %collective-permute-start.3) | collective-permute-done | bytes 65568 | tf_op jit(solution)/shard_map/ppermute | solution.py:178
  12.8 7.0 %tile_best.1 = f32[2,256]{1,0:T(2,128)S(1)} custom-call(s32[2]{0:T(128)S(1)} %pad_add_fusion.bounds, bf16[272,128]{1,0:T(8,128)(2,1)S(1)} %collective-permute-done.1.r_head, bf16[256,128]{1,0:T(8,128)(2,1)S(1)} %get-tuple-element.10.r_tail, bf16[256,128]{1,0:T(8,128)(2,1)S(1)} %add_convert_fusion.c_head, bf16[256,128]{1,0:T(8,128)(2,1)S(1)} %get-tuple-element.9.c_tail), custom_call_target="tpu_custom_call" | custom-call | tf_op jit(solution)/shard_map/tile_best/pallas_call | solution.py:116
  19.7 4.5 %collective-permute-start.4 = (f32[256]{0:T(256)S(1)}, f32[256]{0:T(256)S(1)}, u32[]{:S(2)}, u32[]{:S(2)}) collective-permute-start(f32[256]{0:T(256)S(1)} %bitcast.8), channel_id=1, source_target_pairs={{0,14},{2,0},{4,2},{6,4},{8,6},{10,8},{12,10},{14,12},{1,15},{3,1}... | collective-permute-start | bytes 3080 | tf_op jit(solution)/shard_map/ppermute | solution.py:196
  24.2 1.3 %collective-permute-done.4 = f32[256]{0:T(256)S(1)} collective-permute-done((f32[256]{0:T(256)S(1)}, f32[256]{0:T(256)S(1)}, u32[]{:S(2)}, u32[]{:S(2)}) %collective-permute-start.4) | collective-permute-done | bytes 1056 | tf_op jit(solution)/shard_map/ppermute | solution.py:196
  25.5 0.0 collective-permute-start.5
  25.5 1.1 %collective-permute-done.5 = f32[256]{0:T(256)S(1)} collective-permute-done((f32[256]{0:T(256)S(1)}, f32[256]{0:T(256)S(1)}, u32[]{:S(2)}, u32[]{:S(2)}) %collective-permute-start.5) | collective-permute-done | bytes 1056 | tf_op jit(solution)/shard_map/ppermute | solution.py:178
  26.7 0.6 %max.7 = f32[256]{0:T(256)} maximum(f32[256]{0:T(256)S(1)} %maximum_select_fusion, f32[256]{0:T(256)S(1)} %collective-permute-done.5) | non-fusion elementwise | flops 256 | bytes 3072 | tf_op jit(solution)/shard_map/max | solution.py:198
  (5 shorter events, 0.0 us)
Async XLA Ops:
  1.3 1.5 %collective-permute-start = (f32[256,128]{1,0:T(8,128)S(1)}, f32[256,128]{1,0:T(8,128)S(1)}, u32[]{:S(2)}, u32[]{:S(2)}) collective-permute-start(f32[256,128]{1,0:T(8,128)S(1)} %project.1), channel_id=1, source_target_pairs={{0,1},{1,0},{2,3},{3,2},{4,5},{5,4},{6,7},{7,6},{8,9},{9,8},{10,11... | collective-permute-start | bytes 393224 | tf_op jit(solution)/shard_map/ppermute | solution.py:178
  2.8 8.5 %collective-permute-start.1 = (bf16[272,128]{1,0:T(8,128)(2,1)S(1)}, bf16[272,128]{1,0:T(8,128)(2,1)S(1)}, u32[]{:S(2)}, u32[]{:S(2)}) collective-permute-start(bf16[272,128]{1,0:T(8,128)(2,1)S(1)} %concatenate.3), channel_id=1, source_target_pairs={{14,0},{9,1},{0,2},{11,3},{2,4},{13,5},{4,6},{15,7},{6,8},{1,9},{8... | collective-permute-start | bytes 208904 | tf_op jit(solution)/shard_map/ppermute | solution.py:174
  5.7 5.0 %collective-permute-start.2 = (bf16[256,128]{1,0:T(8,128)(2,1)S(1)}, bf16[256,128]{1,0:T(8,128)(2,1)S(1)}, u32[]{:S(2)}, u32[]{:S(2)}) collective-permute-start(bf16[256,128]{1,0:T(8,128)(2,1)S(1)} %add_convert_fusion.c_head), channel_id=1, source_target_pairs={{2,0},{11,1},{4,2},{13,3},{6,4},{15,5},{8,6},{1,7},{10,8},{3,9},{1... | collective-permute-start | bytes 196616 | tf_op jit(solution)/shard_map/ppermute | solution.py:174
  11.3 1.4 %collective-permute-start.3 = (bf16[256,128]{1,0:T(8,128)(2,1)S(1)}, bf16[256,128]{1,0:T(8,128)(2,1)S(1)}, u32[]{:S(2)}, u32[]{:S(2)}) collective-permute-start(bf16[256,128]{1,0:T(8,128)(2,1)S(1)} %collective-permute-done.2), channel_id=1, source_target_pairs={{0,1},{1,0},{2,3},{3,2},{4,5},{5,4},{6,7},{7,6},{8,9},{9,8},{10,11... | collective-permute-start | bytes 196616 | tf_op jit(solution)/shard_map/ppermute | solution.py:178
  19.7 5.8 %collective-permute-start.4 = (f32[256]{0:T(256)S(1)}, f32[256]{0:T(256)S(1)}, u32[]{:S(2)}, u32[]{:S(2)}) collective-permute-start(f32[256]{0:T(256)S(1)} %bitcast.8), channel_id=1, source_target_pairs={{0,14},{2,0},{4,2},{6,4},{8,6},{10,8},{12,10},{14,12},{1,15},{3,1}... | collective-permute-start | bytes 3080 | tf_op jit(solution)/shard_map/ppermute | solution.py:196
  25.5 1.1 %collective-permute-start.5 = (f32[256]{0:T(256)S(1)}, f32[256]{0:T(256)S(1)}, u32[]{:S(2)}, u32[]{:S(2)}) collective-permute-start(f32[256]{0:T(256)S(1)} %maximum_select_fusion), channel_id=1, source_target_pairs={{0,1},{1,0},{2,3},{3,2},{4,5},{5,4},{6,7},{7,6},{8,9},{9,8},{10,11... | collective-permute-start | bytes 3080 | tf_op jit(solution)/shard_map/ppermute | solution.py:178

commit v5 on v4

--- a/solution.py
+++ b/solution.py
@@ -56,7 +56,7 @@
     in_unit(scoped, (rows, 2 * depth), (0, 1, 0, 1))
 
 
-def tile_kernel(bounds, r_head, r_tail, c_head, c_tail, best, wide, center, inverse):
+def tile_kernel(zone, r_head, r_tail, c_head, c_tail, best, wide, center, inverse):
     rows, depth = c_head.shape
     blocks = rows // BLOCK
     window_stats(((r_head, r_tail), (c_head, c_tail)), wide, center, inverse)
@@ -92,14 +92,16 @@
 
         lax.fori_loop(0, M // SHIFTS, step, 0)
         quarter = rows // 4
-        centre = r_head[rows : rows + 1, 0:1].astype(jnp.float32).astype(jnp.int32)
+        note = r_head[rows : rows + 16, :].astype(jnp.float32).astype(jnp.int32)
+        centre, excluded = note[0:1, 0:1], zone[0:1, 0:1]
+        free = lax.axis_index("chan") * 4 * rows
         found = None
         for block in range(blocks):
             row_pos = block * BLOCK + lax.broadcasted_iota(jnp.int32, (BLOCK, rows), 0)
             col_pos = lax.broadcasted_iota(jnp.int32, (BLOCK, rows), 1)
             diff = col_pos - row_pos
             away = jnp.abs(diff - centre)
-            keep = (away <= quarter + bounds[0]) & (rows + diff >= bounds[1])
+            keep = (away <= quarter + free) & (rows + diff + free >= excluded)
             total = pltpu.matmul_pop(totals[block]) + pltpu.matmul_pop(totals[blocks + block])
             score = jnp.where(keep, total, NEG)
             row_best = jnp.where(diff == 0, jnp.max(score, axis=1, keepdims=True), NEG)
@@ -110,13 +112,13 @@
     in_unit(scoped, (BLOCK, rows), [unit for unit in range(UNITS) for _ in range(blocks)])
 
 
-def tile_best(bounds, r_head, r_tail, c_head, c_tail):
+def tile_best(zone, r_head, r_tail, c_head, c_tail):
     rows, depth = c_head.shape
     vmem = pl.BlockSpec(memory_space=pltpu.VMEM)
     return pl.pallas_call(
         tile_kernel,
         out_shape=jax.ShapeDtypeStruct((2, rows), jnp.float32),
-        in_specs=[pl.BlockSpec(memory_space=pltpu.SMEM), vmem, vmem, vmem, vmem],
+        in_specs=[vmem, vmem, vmem, vmem, vmem],
         out_specs=vmem,
         scratch_shapes=[
             pltpu.VMEM((2, rows + M, depth), jnp.float32),
@@ -125,7 +127,7 @@
         ],
         compiler_params=pltpu.CompilerParams(vmem_limit_bytes=16 << 20),
         name="tile_best",
-    )(bounds, r_head, r_tail, c_head, c_tail)
+    )(zone, r_head, r_tail, c_head, c_tail)
 
 
 def project_kernel(chunk, record, pca_map, partial_sum, samples, weights, arrived):
@@ -191,8 +193,8 @@
     r_head, second = lax.optimization_barrier((r_head, second))
     r_tail = jnp.where(core == 0, proj, second)
     c_tail = jnp.where(core == 0, second, swapped(second))
-    bounds = jnp.stack([core * 4 * rows, exclusion[0] - core * 4 * rows])
-    best = tile_best(bounds, r_head, r_tail, proj, c_tail)
+    zone = jnp.broadcast_to(exclusion[:, None], (8, proj.shape[1]))
+    best = tile_best(zone, r_head, r_tail, proj, c_tail)
     row_back = lax.ppermute(best[1], "tm", [(slab, (slab - 1) % cycle) for slab in range(cycle)])
     own = jnp.where(core == 0, jnp.maximum(best[0], row_back), best[0])
     return jnp.maximum(own, swapped(own))

time: 27.4 us -> 26.8 us (0.978)
  Pallas kernels: 8.23 us -> 7.68 us
    ppermute x2, waiting for transfers between devices: 1.86 us -> 2.51 us  [fetched(): return lax.ppermute(value, ('tm', 'chan'), pairs)]
    ppermute x3, waiting for transfers between devices: 2.29 us -> 1.71 us  [swapped(): return lax.ppermute(value, 'chan', [(0, 1), (1, 0)])]
    pallas_call x1, Pallas kernels: 6.98 us -> 6.43 us  [tile_best(): pl.pallas_call(tile_kernel, out_shape=jax.ShapeDtypeStruct((2, rows), jnp...]
where the time goes in v5:
time: 26.8 us; the launch traced here: 26.7 us
  starting transfers between devices  11.5 us (43%)
  Pallas kernels  7.68 us (29%)
  waiting for transfers between devices  5.52 us (21%)
  between operations  1.35 us (5%)
  other arithmetic  0.6 us (2%)
    pallas_call x1, Pallas kernels, tile_best(): pl.pallas_call(tile_kernel, out_shape=jax.ShapeDtypeStruct((2, rows), jnp...  6.43 us
    ppermute x2, starting transfers between devices, fetched(): return lax.ppermute(value, ('tm', 'chan'), pairs)  6.03 us
    ppermute x1, starting transfers between devices, per_device(): lax.ppermute(best[1], 'tm', [(slab, (slab - 1) % cycle) for slab in range...  4.46 us
    ppermute x2, waiting for transfers between devices, fetched(): return lax.ppermute(value, ('tm', 'chan'), pairs)  2.51 us
    ppermute x3, waiting for transfers between devices, swapped(): return lax.ppermute(value, 'chan', [(0, 1), (1, 0)])  1.71 us
    ppermute x1, waiting for transfers between devices, per_device(): lax.ppermute(best[1], 'tm', [(slab, (slab - 1) % cycle) for slab in range...  1.3 us
    pallas_call x1, Pallas kernels, project(): pl.pallas_call(functools.partial(project_kernel, chunk), out_shape=pltpu....  1.25 us
    ppermute x3, starting transfers between devices, swapped(): return lax.ppermute(value, 'chan', [(0, 1), (1, 0)])  1.02 us
  transfers between devices with their start and end apart: 6, of which 6 were waited for; matrix products, arithmetic and copies ran while one was open for 0% of the time, Pallas kernels for 0%

profile of v5, /device:TPU:0, one launch (start us, length us, event | category | flops | bytes accessed | tf_op | source)
XLA Modules:
  0.0 26.7 jit_solution(2213851790474245910)
XLA Ops:
  0.0 1.3 %project.1 = f32[256,128]{1,0:T(8,128)S(1)} custom-call(bf16[256,512]{1,0:T(8,128)(2,1)} %record.1, bf16[512,128]{1,0:T(8,128)(2,1)} %pca_map.1), custom_call_target="tpu_custom_call" | custom-call | tf_op jit(solution)/shard_map/project/pallas_call | solution.py:154
  1.3 0.5 %collective-permute-start = (f32[256,128]{1,0:T(8,128)S(1)}, f32[256,128]{1,0:T(8,128)S(1)}, u32[]{:S(2)}, u32[]{:S(2)}) collective-permute-start(f32[256,128]{1,0:T(8,128)S(1)} %project.1), channel_id=1, source_target_pairs={{0,1},{1,0},{2,3},{3,2},{4,5},{5,4},{6,7},{7,6},{8,9},{9,8},{10,11... | collective-permute-start | bytes 393224 | tf_op jit(solution)/shard_map/ppermute | solution.py:180
  2.4 0.3 %collective-permute-done = f32[256,128]{1,0:T(8,128)S(1)} collective-permute-done((f32[256,128]{1,0:T(8,128)S(1)}, f32[256,128]{1,0:T(8,128)S(1)}, u32[]{:S(2)}, u32[]{:S(2)}) %collective-permute-start) | collective-permute-done | bytes 131104 | tf_op jit(solution)/shard_map/ppermute | solution.py:180
  2.8 2.9 %collective-permute-start.1 = (bf16[272,128]{1,0:T(8,128)(2,1)S(1)}, bf16[272,128]{1,0:T(8,128)(2,1)S(1)}, u32[]{:S(2)}, u32[]{:S(2)}) collective-permute-start(bf16[272,128]{1,0:T(8,128)(2,1)S(1)} %concatenate.3), channel_id=1, source_target_pairs={{14,0},{9,1},{0,2},{11,3},{2,4},{13,5},{4,6},{15,7},{6,8},{1,9},{8... | collective-permute-start | bytes 208904 | tf_op jit(solution)/shard_map/ppermute | solution.py:176
  5.7 3.1 %collective-permute-start.2 = (bf16[256,128]{1,0:T(8,128)(2,1)S(1)}, bf16[256,128]{1,0:T(8,128)(2,1)S(1)}, u32[]{:S(2)}, u32[]{:S(2)}) collective-permute-start(bf16[256,128]{1,0:T(8,128)(2,1)S(1)} %add_convert_fusion.c_head), channel_id=1, source_target_pairs={{2,0},{11,1},{4,2},{13,3},{6,4},{15,5},{8,6},{1,7},{10,8},{3,9},{1... | collective-permute-start | bytes 196616 | tf_op jit(solution)/shard_map/ppermute | solution.py:176
  8.8 1.9 %collective-permute-done.2 = bf16[256,128]{1,0:T(8,128)(2,1)S(1)} collective-permute-done((bf16[256,128]{1,0:T(8,128)(2,1)S(1)}, bf16[256,128]{1,0:T(8,128)(2,1)S(1)}, u32[]{:S(2)}, u32[]{:S(2)}) %collective-permute-start.2) | collective-permute-done | bytes 65568 | tf_op jit(solution)/shard_map/ppermute | solution.py:176
  10.7 0.6 %collective-permute-done.1.r_head = bf16[272,128]{1,0:T(8,128)(2,1)S(1)} collective-permute-done((bf16[272,128]{1,0:T(8,128)(2,1)S(1)}, bf16[272,128]{1,0:T(8,128)(2,1)S(1)}, u32[]{:S(2)}, u32[]{:S(2)}) %collective-permute-start.1) | collective-permute-done | bytes 69664 | tf_op jit(solution)/shard_map/ppermute | solution.py:176
  11.3 0.5 %collective-permute-start.3 = (bf16[256,128]{1,0:T(8,128)(2,1)S(1)}, bf16[256,128]{1,0:T(8,128)(2,1)S(1)}, u32[]{:S(2)}, u32[]{:S(2)}) collective-permute-start(bf16[256,128]{1,0:T(8,128)(2,1)S(1)} %collective-permute-done.2), channel_id=1, source_target_pairs={{0,1},{1,0},{2,3},{3,2},{4,5},{5,4},{6,7},{7,6},{8,9},{9,8},{10,11... | collective-permute-start | bytes 196616 | tf_op jit(solution)/shard_map/ppermute | solution.py:180
  12.5 0.2 collective-permute-done.3
  12.8 6.4 %tile_best.1 = f32[2,256]{1,0:T(2,128)S(1)} custom-call(s32[8,128]{1,0:T(8,128)S(1)} %broadcast_in_dim.7.zone, bf16[272,128]{1,0:T(8,128)(2,1)S(1)} %collective-permute-done.1.r_head, bf16[256,128]{1,0:T(8,128)(2,1)S(1)} %get-tuple-element.10.r_tail, bf16[256,128]{1,0:T(8,128)(2,1)S(1)} %add_convert_fusion.c_head, bf16[256,128]{1,0:T(8,128)(2,1)S(1)} %get-tuple-element.9.c_tail), custom_call_target="tpu_custom_call" | custom-call | tf_op jit(solution)/shard_map/tile_best/pallas_call | solution.py:118
  19.2 4.5 %collective-permute-start.4 = (f32[256]{0:T(256)S(1)}, f32[256]{0:T(256)S(1)}, u32[]{:S(2)}, u32[]{:S(2)}) collective-permute-start(f32[256]{0:T(256)S(1)} %bitcast.6), channel_id=1, source_target_pairs={{0,14},{2,0},{4,2},{6,4},{8,6},{10,8},{12,10},{14,12},{1,15},{3,1}... | collective-permute-start | bytes 3080 | tf_op jit(solution)/shard_map/ppermute | solution.py:198
  23.7 1.3 %collective-permute-done.4 = f32[256]{0:T(256)S(1)} collective-permute-done((f32[256]{0:T(256)S(1)}, f32[256]{0:T(256)S(1)}, u32[]{:S(2)}, u32[]{:S(2)}) %collective-permute-start.4) | collective-permute-done | bytes 1056 | tf_op jit(solution)/shard_map/ppermute | solution.py:198
  25.0 0.0 collective-permute-start.5
  25.0 1.1 %collective-permute-done.5 = f32[256]{0:T(256)S(1)} collective-permute-done((f32[256]{0:T(256)S(1)}, f32[256]{0:T(256)S(1)}, u32[]{:S(2)}, u32[]{:S(2)}) %collective-permute-start.5) | collective-permute-done | bytes 1056 | tf_op jit(solution)/shard_map/ppermute | solution.py:180
  26.1 0.6 %max.7 = f32[256]{0:T(256)} maximum(f32[256]{0:T(256)S(1)} %maximum_select_fusion, f32[256]{0:T(256)S(1)} %collective-permute-done.5) | non-fusion elementwise | flops 256 | bytes 3072 | tf_op jit(solution)/shard_map/max | solution.py:200
  (6 shorter events, 0.1 us)
Async XLA Ops:
  1.3 1.5 %collective-permute-start = (f32[256,128]{1,0:T(8,128)S(1)}, f32[256,128]{1,0:T(8,128)S(1)}, u32[]{:S(2)}, u32[]{:S(2)}) collective-permute-start(f32[256,128]{1,0:T(8,128)S(1)} %project.1), channel_id=1, source_target_pairs={{0,1},{1,0},{2,3},{3,2},{4,5},{5,4},{6,7},{7,6},{8,9},{9,8},{10,11... | collective-permute-start | bytes 393224 | tf_op jit(solution)/shard_map/ppermute | solution.py:180
  2.8 8.5 %collective-permute-start.1 = (bf16[272,128]{1,0:T(8,128)(2,1)S(1)}, bf16[272,128]{1,0:T(8,128)(2,1)S(1)}, u32[]{:S(2)}, u32[]{:S(2)}) collective-permute-start(bf16[272,128]{1,0:T(8,128)(2,1)S(1)} %concatenate.3), channel_id=1, source_target_pairs={{14,0},{9,1},{0,2},{11,3},{2,4},{13,5},{4,6},{15,7},{6,8},{1,9},{8... | collective-permute-start | bytes 208904 | tf_op jit(solution)/shard_map/ppermute | solution.py:176
  5.7 5.0 %collective-permute-start.2 = (bf16[256,128]{1,0:T(8,128)(2,1)S(1)}, bf16[256,128]{1,0:T(8,128)(2,1)S(1)}, u32[]{:S(2)}, u32[]{:S(2)}) collective-permute-start(bf16[256,128]{1,0:T(8,128)(2,1)S(1)} %add_convert_fusion.c_head), channel_id=1, source_target_pairs={{2,0},{11,1},{4,2},{13,3},{6,4},{15,5},{8,6},{1,7},{10,8},{3,9},{1... | collective-permute-start | bytes 196616 | tf_op jit(solution)/shard_map/ppermute | solution.py:176
  11.3 1.4 %collective-permute-start.3 = (bf16[256,128]{1,0:T(8,128)(2,1)S(1)}, bf16[256,128]{1,0:T(8,128)(2,1)S(1)}, u32[]{:S(2)}, u32[]{:S(2)}) collective-permute-start(bf16[256,128]{1,0:T(8,128)(2,1)S(1)} %collective-permute-done.2), channel_id=1, source_target_pairs={{0,1},{1,0},{2,3},{3,2},{4,5},{5,4},{6,7},{7,6},{8,9},{9,8},{10,11... | collective-permute-start | bytes 196616 | tf_op jit(solution)/shard_map/ppermute | solution.py:180
  19.2 5.8 %collective-permute-start.4 = (f32[256]{0:T(256)S(1)}, f32[256]{0:T(256)S(1)}, u32[]{:S(2)}, u32[]{:S(2)}) collective-permute-start(f32[256]{0:T(256)S(1)} %bitcast.6), channel_id=1, source_target_pairs={{0,14},{2,0},{4,2},{6,4},{8,6},{10,8},{12,10},{14,12},{1,15},{3,1}... | collective-permute-start | bytes 3080 | tf_op jit(solution)/shard_map/ppermute | solution.py:198
  25.0 1.1 %collective-permute-start.5 = (f32[256]{0:T(256)S(1)}, f32[256]{0:T(256)S(1)}, u32[]{:S(2)}, u32[]{:S(2)}) collective-permute-start(f32[256]{0:T(256)S(1)} %maximum_select_fusion), channel_id=1, source_target_pairs={{0,1},{1,0},{2,3},{3,2},{4,5},{5,4},{6,7},{7,6},{8,9},{9,8},{10,11... | collective-permute-start | bytes 3080 | tf_op jit(solution)/shard_map/ppermute | solution.py:180

commit v6 on v5

--- a/solution.py
+++ b/solution.py
@@ -166,13 +166,10 @@
     )(*(pltpu.with_memory_space_constraint(x, pltpu.HBM) for x in (record, pca_map)))
 
 
-def fetched(value, near_steps, far_steps):
-    cycle = lax.axis_size("tm")
+def fetched(value, near, far):
     pairs = []
-    for slab in range(cycle):
-        for core, steps in ((0, near_steps), (1, far_steps)):
-            if steps is not None:
-                pairs.append(((slab + steps) % cycle * 2 + core, slab * 2 + core))
+    for slab in range(lax.axis_size("tm")):
+        pairs += [(near[slab] * 2, slab * 2), (far[slab] * 2 + 1, slab * 2 + 1)]
     return lax.ppermute(value, ("tm", "chan"), pairs)
 
 
@@ -188,14 +185,18 @@
     proj = (partial_value + swapped(partial_value)).astype(jnp.bfloat16)
     note = jnp.broadcast_to(offsets.astype(jnp.bfloat16)[:, None], (16, proj.shape[1]))
     noted = jnp.concatenate([proj, note], axis=0)
-    r_head = fetched(noted, -1, cycle // 2)
-    second = fetched(proj, 1, cycle // 2 + 1)
-    r_head, second = lax.optimization_barrier((r_head, second))
+    half = cycle // 2
+    turns = range(cycle)
+    beside = [turn ^ 1 for turn in turns]
+    r_head = fetched(noted, [(turn - 1) % cycle for turn in turns], [(turn + half) % cycle for turn in turns])
+    second = fetched(proj, [(turn + 1) % cycle for turn in turns], [(turn + half + 1) % cycle for turn in turns])
+    third = fetched(proj, beside, [(turn + 1) % cycle for turn in turns])
+    r_head, second, third = lax.optimization_barrier((r_head, second, third))
     r_tail = jnp.where(core == 0, proj, second)
-    c_tail = jnp.where(core == 0, second, swapped(second))
+    c_tail = jnp.where(core == 0, second, third)
     zone = jnp.broadcast_to(exclusion[:, None], (8, proj.shape[1]))
     best = tile_best(zone, r_head, r_tail, proj, c_tail)
-    row_back = lax.ppermute(best[1], "tm", [(slab, (slab - 1) % cycle) for slab in range(cycle)])
+    row_back = fetched(best[1], [(turn + 1) % cycle for turn in turns], beside)
     own = jnp.where(core == 0, jnp.maximum(best[0], row_back), best[0])
     return jnp.maximum(own, swapped(own))
 

time: 26.8 us -> 25.6 us (0.955)
  starting transfers between devices: 11.5 us -> 9.08 us
  waiting for transfers between devices: 5.52 us -> 6.7 us
    ppermute x1 -> x0, starting transfers between devices: 4.46 us -> none  [per_device(): lax.ppermute(best[1], 'tm', [(slab, (slab - 1) % cycle) for slab in range...]
    ppermute x2 -> x4, waiting for transfers between devices: 2.51 us -> 5.23 us  [fetched(): return lax.ppermute(value, ('tm', 'chan'), pairs)]
    ppermute x2 -> x4, starting transfers between devices: 6.03 us -> 8.56 us  [fetched(): return lax.ppermute(value, ('tm', 'chan'), pairs)]
    ppermute x1 -> x0, waiting for transfers between devices: 1.3 us -> none  [per_device(): lax.ppermute(best[1], 'tm', [(slab, (slab - 1) % cycle) for slab in range...]
    ppermute x3 -> x2, starting transfers between devices: 1.02 us -> 0.52 us  [swapped(): return lax.ppermute(value, 'chan', [(0, 1), (1, 0)])]
    ppermute x3 -> x2, waiting for transfers between devices: 1.71 us -> 1.47 us  [swapped(): return lax.ppermute(value, 'chan', [(0, 1), (1, 0)])]
  transfers between devices with their start and end apart: 6 -> 6, of which waited for: 6 -> 5; matrix products, arithmetic and copies ran while one was open for 0% -> 0% of each run, Pallas kernels for 0% -> 0%
where the time goes in v6:
time: 25.6 us; the launch traced here: 25.4 us
  starting transfers between devices  9.08 us (35%)
  Pallas kernels  7.69 us (30%)
  waiting for transfers between devices  6.7 us (26%)
  between operations  1.35 us (5%)
  other arithmetic  0.6 us (2%)
    ppermute x4, starting transfers between devices, fetched(): return lax.ppermute(value, ('tm', 'chan'), pairs)  8.56 us
    pallas_call x1, Pallas kernels, tile_best(): pl.pallas_call(tile_kernel, out_shape=jax.ShapeDtypeStruct((2, rows), jnp...  6.43 us
    ppermute x4, waiting for transfers between devices, fetched(): return lax.ppermute(value, ('tm', 'chan'), pairs)  5.23 us
    ppermute x2, waiting for transfers between devices, swapped(): return lax.ppermute(value, 'chan', [(0, 1), (1, 0)])  1.47 us
    pallas_call x1, Pallas kernels, project(): pl.pallas_call(functools.partial(project_kernel, chunk), out_shape=pltpu....  1.25 us
    max x1, other arithmetic, per_device(): return jnp.maximum(own, swapped(own))  0.56 us
    ppermute x2, starting transfers between devices, swapped(): return lax.ppermute(value, 'chan', [(0, 1), (1, 0)])  0.52 us
  transfers between devices with their start and end apart: 6, of which 5 were waited for; matrix products, arithmetic and copies ran while one was open for 0% of the time, Pallas kernels for 0%

profile of v6, /device:TPU:0, one launch (start us, length us, event | category | flops | bytes accessed | tf_op | source)
XLA Modules:
  0.0 25.4 jit_solution(3599948363740395656)
XLA Ops:
  0.0 1.3 %project.1 = f32[256,128]{1,0:T(8,128)S(1)} custom-call(bf16[256,512]{1,0:T(8,128)(2,1)} %record.1, bf16[512,128]{1,0:T(8,128)(2,1)} %pca_map.1), custom_call_target="tpu_custom_call" | custom-call | tf_op jit(solution)/shard_map/project/pallas_call | solution.py:154
  1.3 0.5 %collective-permute-start = (f32[256,128]{1,0:T(8,128)S(1)}, f32[256,128]{1,0:T(8,128)S(1)}, u32[]{:S(2)}, u32[]{:S(2)}) collective-permute-start(f32[256,128]{1,0:T(8,128)S(1)} %project.1), channel_id=1, source_target_pairs={{0,1},{1,0},{2,3},{3,2},{4,5},{5,4},{6,7},{7,6},{8,9},{9,8},{10,11... | collective-permute-start | bytes 393224 | tf_op jit(solution)/shard_map/ppermute | solution.py:177
  2.4 0.3 %collective-permute-done = f32[256,128]{1,0:T(8,128)S(1)} collective-permute-done((f32[256,128]{1,0:T(8,128)S(1)}, f32[256,128]{1,0:T(8,128)S(1)}, u32[]{:S(2)}, u32[]{:S(2)}) %collective-permute-start) | collective-permute-done | bytes 131104 | tf_op jit(solution)/shard_map/ppermute | solution.py:177
  2.8 2.9 %collective-permute-start.1 = (bf16[272,128]{1,0:T(8,128)(2,1)S(1)}, bf16[272,128]{1,0:T(8,128)(2,1)S(1)}, u32[]{:S(2)}, u32[]{:S(2)}) collective-permute-start(bf16[272,128]{1,0:T(8,128)(2,1)S(1)} %concatenate.3), channel_id=1, source_target_pairs={{14,0},{9,1},{0,2},{11,3},{2,4},{13,5},{4,6},{15,7},{6,8},{1,9},{8... | collective-permute-start | bytes 208904 | tf_op jit(solution)/shard_map/ppermute | solution.py:173
  5.7 3.1 %collective-permute-start.2 = (bf16[256,128]{1,0:T(8,128)(2,1)S(1)}, bf16[256,128]{1,0:T(8,128)(2,1)S(1)}, u32[]{:S(2)}, u32[]{:S(2)}) collective-permute-start(bf16[256,128]{1,0:T(8,128)(2,1)S(1)} %add_convert_fusion.c_head), channel_id=1, source_target_pairs={{2,0},{11,1},{4,2},{13,3},{6,4},{15,5},{8,6},{1,7},{10,8},{3,9},{1... | collective-permute-start | bytes 196616 | tf_op jit(solution)/shard_map/ppermute | solution.py:173
  8.8 0.0 collective-permute-start.3
  9.5 1.2 %collective-permute-done.2 = bf16[256,128]{1,0:T(8,128)(2,1)S(1)} collective-permute-done((bf16[256,128]{1,0:T(8,128)(2,1)S(1)}, bf16[256,128]{1,0:T(8,128)(2,1)S(1)}, u32[]{:S(2)}, u32[]{:S(2)}) %collective-permute-start.2) | collective-permute-done | bytes 65568 | tf_op jit(solution)/shard_map/ppermute | solution.py:173
  10.7 2.7 %collective-permute-done.3 = bf16[256,128]{1,0:T(8,128)(2,1)S(1)} collective-permute-done((bf16[256,128]{1,0:T(8,128)(2,1)S(1)}, bf16[256,128]{1,0:T(8,128)(2,1)S(1)}, u32[]{:S(2)}, u32[]{:S(2)}) %collective-permute-start.3) | collective-permute-done | bytes 65568 | tf_op jit(solution)/shard_map/ppermute | solution.py:173
  13.4 0.0 collective-permute-done.1.r_head
  13.5 6.4 %tile_best.1 = f32[2,256]{1,0:T(2,128)S(1)} custom-call(s32[8,128]{1,0:T(8,128)S(1)} %broadcast_in_dim.7.zone, bf16[272,128]{1,0:T(8,128)(2,1)S(1)} %collective-permute-done.1.r_head, bf16[256,128]{1,0:T(8,128)(2,1)S(1)} %get-tuple-element.12.r_tail, bf16[256,128]{1,0:T(8,128)(2,1)S(1)} %add_convert_fusion.c_head, bf16[256,128]{1,0:T(8,128)(2,1)S(1)} %get-tuple-element.11.c_tail), custom_call_target="tpu_custom_call" | custom-call | tf_op jit(solution)/shard_map/tile_best/pallas_call | solution.py:118
  19.9 2.5 %collective-permute-start.4 = (f32[256]{0:T(256)S(1)}, f32[256]{0:T(256)S(1)}, u32[]{:S(2)}, u32[]{:S(2)}) collective-permute-start(f32[256]{0:T(256)S(1)} %bitcast.6), channel_id=1, source_target_pairs={{2,0},{3,1},{4,2},{1,3},{6,4},{7,5},{8,6},{5,7},{10,8},{11,9},{12,... | collective-permute-start | bytes 3080 | tf_op jit(solution)/shard_map/ppermute | solution.py:173
  22.4 1.3 %collective-permute-done.4 = f32[256]{0:T(256)S(1)} collective-permute-done((f32[256]{0:T(256)S(1)}, f32[256]{0:T(256)S(1)}, u32[]{:S(2)}, u32[]{:S(2)}) %collective-permute-start.4) | collective-permute-done | bytes 1056 | tf_op jit(solution)/shard_map/ppermute | solution.py:173
  23.7 0.0 collective-permute-start.5
  23.7 1.1 %collective-permute-done.5 = f32[256]{0:T(256)S(1)} collective-permute-done((f32[256]{0:T(256)S(1)}, f32[256]{0:T(256)S(1)}, u32[]{:S(2)}, u32[]{:S(2)}) %collective-permute-start.5) | collective-permute-done | bytes 1056 | tf_op jit(solution)/shard_map/ppermute | solution.py:177
  24.9 0.6 %max.7 = f32[256]{0:T(256)} maximum(f32[256]{0:T(256)S(1)} %maximum_select_fusion, f32[256]{0:T(256)S(1)} %collective-permute-done.5) | non-fusion elementwise | flops 256 | bytes 3072 | tf_op jit(solution)/shard_map/max | solution.py:201
  (6 shorter events, 0.1 us)
Async XLA Ops:
  1.3 1.5 %collective-permute-start = (f32[256,128]{1,0:T(8,128)S(1)}, f32[256,128]{1,0:T(8,128)S(1)}, u32[]{:S(2)}, u32[]{:S(2)}) collective-permute-start(f32[256,128]{1,0:T(8,128)S(1)} %project.1), channel_id=1, source_target_pairs={{0,1},{1,0},{2,3},{3,2},{4,5},{5,4},{6,7},{7,6},{8,9},{9,8},{10,11... | collective-permute-start | bytes 393224 | tf_op jit(solution)/shard_map/ppermute | solution.py:177
  2.8 10.6 %collective-permute-start.1 = (bf16[272,128]{1,0:T(8,128)(2,1)S(1)}, bf16[272,128]{1,0:T(8,128)(2,1)S(1)}, u32[]{:S(2)}, u32[]{:S(2)}) collective-permute-start(bf16[272,128]{1,0:T(8,128)(2,1)S(1)} %concatenate.3), channel_id=1, source_target_pairs={{14,0},{9,1},{0,2},{11,3},{2,4},{13,5},{4,6},{15,7},{6,8},{1,9},{8... | collective-permute-start | bytes 208904 | tf_op jit(solution)/shard_map/ppermute | solution.py:173
  5.7 5.0 %collective-permute-start.2 = (bf16[256,128]{1,0:T(8,128)(2,1)S(1)}, bf16[256,128]{1,0:T(8,128)(2,1)S(1)}, u32[]{:S(2)}, u32[]{:S(2)}) collective-permute-start(bf16[256,128]{1,0:T(8,128)(2,1)S(1)} %add_convert_fusion.c_head), channel_id=1, source_target_pairs={{2,0},{11,1},{4,2},{13,3},{6,4},{15,5},{8,6},{1,7},{10,8},{3,9},{1... | collective-permute-start | bytes 196616 | tf_op jit(solution)/shard_map/ppermute | solution.py:173
  8.8 4.6 %collective-permute-start.3 = (bf16[256,128]{1,0:T(8,128)(2,1)S(1)}, bf16[256,128]{1,0:T(8,128)(2,1)S(1)}, u32[]{:S(2)}, u32[]{:S(2)}) collective-permute-start(bf16[256,128]{1,0:T(8,128)(2,1)S(1)} %add_convert_fusion.c_head), channel_id=1, source_target_pairs={{2,0},{3,1},{0,2},{5,3},{6,4},{7,5},{4,6},{9,7},{10,8},{11,9},{8,1... | collective-permute-start | bytes 196616 | tf_op jit(solution)/shard_map/ppermute | solution.py:173
  19.9 3.8 %collective-permute-start.4 = (f32[256]{0:T(256)S(1)}, f32[256]{0:T(256)S(1)}, u32[]{:S(2)}, u32[]{:S(2)}) collective-permute-start(f32[256]{0:T(256)S(1)} %bitcast.6), channel_id=1, source_target_pairs={{2,0},{3,1},{4,2},{1,3},{6,4},{7,5},{8,6},{5,7},{10,8},{11,9},{12,... | collective-permute-start | bytes 3080 | tf_op jit(solution)/shard_map/ppermute | solution.py:173
  23.7 1.1 %collective-permute-start.5 = (f32[256]{0:T(256)S(1)}, f32[256]{0:T(256)S(1)}, u32[]{:S(2)}, u32[]{:S(2)}) collective-permute-start(f32[256]{0:T(256)S(1)} %maximum_select_fusion), channel_id=1, source_target_pairs={{0,1},{1,0},{2,3},{3,2},{4,5},{5,4},{6,7},{7,6},{8,9},{9,8},{10,11... | collective-permute-start | bytes 3080 | tf_op jit(solution)/shard_map/ppermute | solution.py:177

commit v7 on v6

--- a/solution.py
+++ b/solution.py
@@ -20,7 +20,7 @@
 
 
 def window_stats(sides, wide, center, inverse):
-    rows, depth = sides[1][0].shape
+    rows, depth = sides[0][1].shape
     scale = float(M * depth) ** 0.25
     row_pos = lax.broadcasted_iota(jnp.int32, (rows, rows), 0)
     col_pos = lax.broadcasted_iota(jnp.int32, (rows, rows), 1)
@@ -57,7 +57,7 @@
 
 
 def tile_kernel(zone, r_head, r_tail, c_head, c_tail, best, wide, center, inverse):
-    rows, depth = c_head.shape
+    rows, depth = r_tail.shape
     blocks = rows // BLOCK
     window_stats(((r_head, r_tail), (c_head, c_tail)), wide, center, inverse)
 
@@ -92,16 +92,20 @@
 
         lax.fori_loop(0, M // SHIFTS, step, 0)
         quarter = rows // 4
-        note = r_head[rows : rows + 16, :].astype(jnp.float32).astype(jnp.int32)
-        centre, excluded = note[0:1, 0:1], zone[0:1, 0:1]
-        free = lax.axis_index("chan") * 4 * rows
+        core = lax.axis_index("chan")
+        edge = core * (lax.axis_index("tm") == lax.axis_size("tm") - 1).astype(jnp.int32)
+        notes = [head[rows : rows + 16, :].astype(jnp.float32)[0:1, 0:1] for head in (r_head, c_head)]
+        centre = jnp.where(core == 0, *notes).astype(jnp.int32)
+        excluded = zone[0:1, 0:1]
+        free = (core - edge) * 4 * rows
         found = None
         for block in range(blocks):
             row_pos = block * BLOCK + lax.broadcasted_iota(jnp.int32, (BLOCK, rows), 0)
             col_pos = lax.broadcasted_iota(jnp.int32, (BLOCK, rows), 1)
             diff = col_pos - row_pos
-            away = jnp.abs(diff - centre)
-            keep = (away <= quarter + free) & (rows + diff + free >= excluded)
+            ahead = diff * (1 - 2 * edge)
+            away = jnp.abs(ahead - centre)
+            keep = (away <= quarter + free) & (rows + ahead + free >= excluded)
             total = pltpu.matmul_pop(totals[block]) + pltpu.matmul_pop(totals[blocks + block])
             score = jnp.where(keep, total, NEG)
             row_best = jnp.where(diff == 0, jnp.max(score, axis=1, keepdims=True), NEG)
@@ -113,7 +117,7 @@
 
 
 def tile_best(zone, r_head, r_tail, c_head, c_tail):
-    rows, depth = c_head.shape
+    rows, depth = r_tail.shape
     vmem = pl.BlockSpec(memory_space=pltpu.VMEM)
     return pl.pallas_call(
         tile_kernel,
@@ -166,10 +170,10 @@
     )(*(pltpu.with_memory_space_constraint(x, pltpu.HBM) for x in (record, pca_map)))
 
 
-def fetched(value, near, far):
+def fetched(value, sources):
     pairs = []
-    for slab in range(lax.axis_size("tm")):
-        pairs += [(near[slab] * 2, slab * 2), (far[slab] * 2 + 1, slab * 2 + 1)]
+    for slab, both in enumerate(sources):
+        pairs += [(2 * turn + core, 2 * slab + place) for place, (turn, core) in enumerate(both)]
     return lax.ppermute(value, ("tm", "chan"), pairs)
 
 
@@ -187,17 +191,26 @@
     noted = jnp.concatenate([proj, note], axis=0)
     half = cycle // 2
     turns = range(cycle)
-    beside = [turn ^ 1 for turn in turns]
-    r_head = fetched(noted, [(turn - 1) % cycle for turn in turns], [(turn + half) % cycle for turn in turns])
-    second = fetched(proj, [(turn + 1) % cycle for turn in turns], [(turn + half + 1) % cycle for turn in turns])
-    third = fetched(proj, beside, [(turn + 1) % cycle for turn in turns])
+    last = cycle - 1
+    edge = (core == 1) & (lax.axis_index("tm") == last)
+    first = [(((turn - 1) % cycle, 0), ((turn + half) % cycle, 1)) for turn in turns]
+    second = [((turn + 1, 0), ((turn + half + 1) % cycle, 1)) for turn in turns[:-1]] + [((0, 0), (1, 0))]
+    second[0] = ((half, 1), second[0][1])
+    third = [((turn, 1), ((turn + 1) % cycle, 0)) for turn in turns]
+    third[0], third[1] = ((1, 1), (1, 0)), ((0, 1), third[1][1])
+    r_head, second, third = [fetched(noted, first), fetched(proj, second), fetched(proj, third)]
     r_head, second, third = lax.optimization_barrier((r_head, second, third))
+    r_head = jnp.where(edge, jnp.concatenate([third, note], axis=0), r_head)
     r_tail = jnp.where(core == 0, proj, second)
-    c_tail = jnp.where(core == 0, second, third)
+    c_tail = jnp.where((core == 1) | (lax.axis_index("tm") == 0), third[:rows], second)
     zone = jnp.broadcast_to(exclusion[:, None], (8, proj.shape[1]))
-    best = tile_best(zone, r_head, r_tail, proj, c_tail)
-    row_back = fetched(best[1], [(turn + 1) % cycle for turn in turns], beside)
-    own = jnp.where(core == 0, jnp.maximum(best[0], row_back), best[0])
+    best = tile_best(zone, r_head, r_tail, noted, c_tail)
+    beyond = [(turn - 1, 1) for turn in turns]
+    beyond[0], beyond[half], beyond[last] = (0, 0), (last - 1, 1), (half - 1, 1)
+    back = [((turn + 1, 0), beyond[turn]) for turn in turns[:-1]] + [((last, 1), beyond[last])]
+    back = fetched(best[1], back)
+    wanted = jnp.where(core == 0, lax.axis_index("tm") != last, edge)
+    own = jnp.where(wanted, jnp.maximum(best[0], back), best[0])
     return jnp.maximum(own, swapped(own))
 
 

time: 25.6 us -> 25.4 us (level)
  starting transfers between devices: 9.08 us -> 8.71 us
    ppermute x4, starting transfers between devices: 8.56 us -> 8.19 us  [fetched(): return lax.ppermute(value, ('tm', 'chan'), pairs)]
  transfers between devices with their start and end apart: 6 -> 6, of which waited for: 5 -> 4; matrix products, arithmetic and copies ran while one was open for 0% -> 0% of each run, Pallas kernels for 0% -> 0%
where the time goes in v7:
time: 25.4 us; the launch traced here: 25.2 us
  starting transfers between devices  8.71 us (34%)
  Pallas kernels  7.69 us (30%)
  waiting for transfers between devices  6.79 us (27%)
  between operations  1.36 us (5%)
  other arithmetic  0.63 us (2%)
    ppermute x4, starting transfers between devices, fetched(): return lax.ppermute(value, ('tm', 'chan'), pairs)  8.19 us
    pallas_call x1, Pallas kernels, tile_best(): pl.pallas_call(tile_kernel, out_shape=jax.ShapeDtypeStruct((2, rows), jnp...  6.44 us
    ppermute x4, waiting for transfers between devices, fetched(): return lax.ppermute(value, ('tm', 'chan'), pairs)  5.32 us
    ppermute x2, waiting for transfers between devices, swapped(): return lax.ppermute(value, 'chan', [(0, 1), (1, 0)])  1.47 us
    pallas_call x1, Pallas kernels, project(): pl.pallas_call(functools.partial(project_kernel, chunk), out_shape=pltpu....  1.25 us
    max x1, other arithmetic, per_device(): return jnp.maximum(own, swapped(own))  0.56 us
    ppermute x2, starting transfers between devices, swapped(): return lax.ppermute(value, 'chan', [(0, 1), (1, 0)])  0.52 us
  transfers between devices with their start and end apart: 6, of which 4 were waited for; matrix products, arithmetic and copies ran while one was open for 0% of the time, Pallas kernels for 0%

profile of v7, /device:TPU:0, one launch (start us, length us, event | category | flops | bytes accessed | tf_op | source)
XLA Modules:
  0.0 25.2 jit_solution(767629880034792960)
XLA Ops:
  0.0 1.3 %project.1 = f32[256,128]{1,0:T(8,128)S(1)} custom-call(bf16[256,512]{1,0:T(8,128)(2,1)} %record.1, bf16[512,128]{1,0:T(8,128)(2,1)} %pca_map.1), custom_call_target="tpu_custom_call" | custom-call | tf_op jit(solution)/shard_map/project/pallas_call | solution.py:158
  1.3 0.5 %collective-permute-start = (f32[256,128]{1,0:T(8,128)S(1)}, f32[256,128]{1,0:T(8,128)S(1)}, u32[]{:S(2)}, u32[]{:S(2)}) collective-permute-start(f32[256,128]{1,0:T(8,128)S(1)} %project.1), channel_id=1, source_target_pairs={{0,1},{1,0},{2,3},{3,2},{4,5},{5,4},{6,7},{7,6},{8,9},{9,8},{10,11... | collective-permute-start | bytes 393224 | tf_op jit(solution)/shard_map/ppermute | solution.py:181
  2.4 0.3 %collective-permute-done = f32[256,128]{1,0:T(8,128)S(1)} collective-permute-done((f32[256,128]{1,0:T(8,128)S(1)}, f32[256,128]{1,0:T(8,128)S(1)}, u32[]{:S(2)}, u32[]{:S(2)}) %collective-permute-start) | collective-permute-done | bytes 131104 | tf_op jit(solution)/shard_map/ppermute | solution.py:181
  2.8 2.9 %collective-permute-start.1 = (bf16[272,128]{1,0:T(8,128)(2,1)S(1)}, bf16[272,128]{1,0:T(8,128)(2,1)S(1)}, u32[]{:S(2)}, u32[]{:S(2)}) collective-permute-start(bf16[272,128]{1,0:T(8,128)(2,1)S(1)} %concatenate.6.c_head), channel_id=1, source_target_pairs={{14,0},{9,1},{0,2},{11,3},{2,4},{13,5},{4,6},{15,7},{6,8},{1,9},{8... | collective-permute-start | bytes 208904 | tf_op jit(solution)/shard_map/ppermute | solution.py:177
  5.7 3.1 %collective-permute-start.2 = (bf16[256,128]{1,0:T(8,128)(2,1)S(1)}, bf16[256,128]{1,0:T(8,128)(2,1)S(1)}, u32[]{:S(2)}, u32[]{:S(2)}) collective-permute-start(bf16[256,128]{1,0:T(8,128)(2,1)S(1)} %add_convert_fusion), channel_id=1, source_target_pairs={{9,0},{11,1},{4,2},{13,3},{6,4},{15,5},{8,6},{1,7},{10,8},{3,9},{1... | collective-permute-start | bytes 196616 | tf_op jit(solution)/shard_map/ppermute | solution.py:177
  8.8 2.0 %collective-permute-start.3 = (bf16[256,128]{1,0:T(8,128)(2,1)S(1)}, bf16[256,128]{1,0:T(8,128)(2,1)S(1)}, u32[]{:S(2)}, u32[]{:S(2)}) collective-permute-start(bf16[256,128]{1,0:T(8,128)(2,1)S(1)} %add_convert_fusion), channel_id=1, source_target_pairs={{3,0},{2,1},{1,2},{4,3},{5,4},{6,5},{7,6},{8,7},{9,8},{10,9},{11,1... | collective-permute-start | bytes 196616 | tf_op jit(solution)/shard_map/ppermute | solution.py:177
  11.5 0.0 collective-permute-done.2
  11.5 1.9 %collective-permute-done.3 = bf16[256,128]{1,0:T(8,128)(2,1)S(1)} collective-permute-done((bf16[256,128]{1,0:T(8,128)(2,1)S(1)}, bf16[256,128]{1,0:T(8,128)(2,1)S(1)}, u32[]{:S(2)}, u32[]{:S(2)}) %collective-permute-start.3) | collective-permute-done | bytes 65568 | tf_op jit(solution)/shard_map/ppermute | solution.py:177
  13.3 0.0 collective-permute-done.1
  13.4 6.4 %tile_best.1 = f32[2,256]{1,0:T(2,128)S(1)} custom-call(s32[8,128]{1,0:T(8,128)S(1)} %broadcast_in_dim.7.zone, bf16[272,128]{1,0:T(8,128)(2,1)S(1)} %pad_select_fusion.r_head, bf16[256,128]{1,0:T(8,128)(2,1)S(1)} %get-tuple-element.12.r_tail, bf16[272,128]{1,0:T(8,128)(2,1)S(1)} %concatenate.6.c_head, bf16[256,128]{1,0:T(8,128)(2,1)S(1)} %get-tuple-element.11.c_tail), custom_call_target="tpu_custom_call" | custom-call | tf_op jit(solution)/shard_map/tile_best/pallas_call | solution.py:122
  19.9 0.2 collective-permute-start.4
  20.0 3.5 %collective-permute-done.4 = f32[256]{0:T(256)S(1)} collective-permute-done((f32[256]{0:T(256)S(1)}, f32[256]{0:T(256)S(1)}, u32[]{:S(2)}, u32[]{:S(2)}) %collective-permute-start.4) | collective-permute-done | bytes 1056 | tf_op jit(solution)/shard_map/ppermute | solution.py:177
  23.5 0.0 collective-permute-start.5
  23.5 1.1 %collective-permute-done.5 = f32[256]{0:T(256)S(1)} collective-permute-done((f32[256]{0:T(256)S(1)}, f32[256]{0:T(256)S(1)}, u32[]{:S(2)}, u32[]{:S(2)}) %collective-permute-start.5) | collective-permute-done | bytes 1056 | tf_op jit(solution)/shard_map/ppermute | solution.py:181
  24.6 0.6 %max.7 = f32[256]{0:T(256)} maximum(f32[256]{0:T(256)S(1)} %maximum_select_fusion, f32[256]{0:T(256)S(1)} %collective-permute-done.5) | non-fusion elementwise | flops 256 | bytes 3072 | tf_op jit(solution)/shard_map/max | solution.py:214
  (7 shorter events, 0.1 us)
Async XLA Ops:
  1.3 1.5 %collective-permute-start = (f32[256,128]{1,0:T(8,128)S(1)}, f32[256,128]{1,0:T(8,128)S(1)}, u32[]{:S(2)}, u32[]{:S(2)}) collective-permute-start(f32[256,128]{1,0:T(8,128)S(1)} %project.1), channel_id=1, source_target_pairs={{0,1},{1,0},{2,3},{3,2},{4,5},{5,4},{6,7},{7,6},{8,9},{9,8},{10,11... | collective-permute-start | bytes 393224 | tf_op jit(solution)/shard_map/ppermute | solution.py:181
  2.8 10.6 %collective-permute-start.1 = (bf16[272,128]{1,0:T(8,128)(2,1)S(1)}, bf16[272,128]{1,0:T(8,128)(2,1)S(1)}, u32[]{:S(2)}, u32[]{:S(2)}) collective-permute-start(bf16[272,128]{1,0:T(8,128)(2,1)S(1)} %concatenate.6.c_head), channel_id=1, source_target_pairs={{14,0},{9,1},{0,2},{11,3},{2,4},{13,5},{4,6},{15,7},{6,8},{1,9},{8... | collective-permute-start | bytes 208904 | tf_op jit(solution)/shard_map/ppermute | solution.py:177
  5.7 5.7 %collective-permute-start.2 = (bf16[256,128]{1,0:T(8,128)(2,1)S(1)}, bf16[256,128]{1,0:T(8,128)(2,1)S(1)}, u32[]{:S(2)}, u32[]{:S(2)}) collective-permute-start(bf16[256,128]{1,0:T(8,128)(2,1)S(1)} %add_convert_fusion), channel_id=1, source_target_pairs={{9,0},{11,1},{4,2},{13,3},{6,4},{15,5},{8,6},{1,7},{10,8},{3,9},{1... | collective-permute-start | bytes 196616 | tf_op jit(solution)/shard_map/ppermute | solution.py:177
  8.8 4.5 %collective-permute-start.3 = (bf16[256,128]{1,0:T(8,128)(2,1)S(1)}, bf16[256,128]{1,0:T(8,128)(2,1)S(1)}, u32[]{:S(2)}, u32[]{:S(2)}) collective-permute-start(bf16[256,128]{1,0:T(8,128)(2,1)S(1)} %add_convert_fusion), channel_id=1, source_target_pairs={{3,0},{2,1},{1,2},{4,3},{5,4},{6,5},{7,6},{8,7},{9,8},{10,9},{11,1... | collective-permute-start | bytes 196616 | tf_op jit(solution)/shard_map/ppermute | solution.py:177
  19.9 3.6 %collective-permute-start.4 = (f32[256]{0:T(256)S(1)}, f32[256]{0:T(256)S(1)}, u32[]{:S(2)}, u32[]{:S(2)}) collective-permute-start(f32[256]{0:T(256)S(1)} %bitcast.6), channel_id=1, source_target_pairs={{2,0},{0,1},{4,2},{1,3},{6,4},{3,5},{8,6},{5,7},{10,8},{13,9},{12,... | collective-permute-start | bytes 3080 | tf_op jit(solution)/shard_map/ppermute | solution.py:177
  23.5 1.1 %collective-permute-start.5 = (f32[256]{0:T(256)S(1)}, f32[256]{0:T(256)S(1)}, u32[]{:S(2)}, u32[]{:S(2)}) collective-permute-start(f32[256]{0:T(256)S(1)} %maximum_select_fusion), channel_id=1, source_target_pairs={{0,1},{1,0},{2,3},{3,2},{4,5},{5,4},{6,7},{7,6},{8,9},{9,8},{10,11... | collective-permute-start | bytes 3080 | tf_op jit(solution)/shard_map/ppermute | solution.py:181

commit v8 on v7

--- a/solution.py
+++ b/solution.py
@@ -194,15 +194,15 @@
     last = cycle - 1
     edge = (core == 1) & (lax.axis_index("tm") == last)
     first = [(((turn - 1) % cycle, 0), ((turn + half) % cycle, 1)) for turn in turns]
-    second = [((turn + 1, 0), ((turn + half + 1) % cycle, 1)) for turn in turns[:-1]] + [((0, 0), (1, 0))]
-    second[0] = ((half, 1), second[0][1])
-    third = [((turn, 1), ((turn + 1) % cycle, 0)) for turn in turns]
-    third[0], third[1] = ((1, 1), (1, 0)), ((0, 1), third[1][1])
+    second = [((turn + 1, 0), ((turn + half + 1) % cycle, 1)) for turn in turns[:-1]] + [((half, 1), (0, 0))]
+    third = [((turn, 1), (turn + 1, 0)) for turn in turns[:-1]] + [((0, 0), (1, 1))]
+    for turn in range(1, last, 2):
+        third[turn] = ((turn + 2, 1), third[turn][1])
     r_head, second, third = [fetched(noted, first), fetched(proj, second), fetched(proj, third)]
     r_head, second, third = lax.optimization_barrier((r_head, second, third))
-    r_head = jnp.where(edge, jnp.concatenate([third, note], axis=0), r_head)
-    r_tail = jnp.where(core == 0, proj, second)
-    c_tail = jnp.where((core == 1) | (lax.axis_index("tm") == 0), third[:rows], second)
+    r_head = jnp.where(edge, jnp.concatenate([second, note], axis=0), r_head)
+    r_tail = jnp.where(core == 0, proj, jnp.where(edge, third, second))
+    c_tail = jnp.where((core == 1) ^ (lax.axis_index("tm") == last), third, second)
     zone = jnp.broadcast_to(exclusion[:, None], (8, proj.shape[1]))
     best = tile_best(zone, r_head, r_tail, noted, c_tail)
     beyond = [(turn - 1, 1) for turn in turns]

time: 25.4 us -> 24.7 us (0.972)
  waiting for transfers between devices: 6.79 us -> 6.26 us
    ppermute x4, waiting for transfers between devices: 5.32 us -> 4.79 us  [fetched(): return lax.ppermute(value, ('tm', 'chan'), pairs)]
where the time goes in v8:
time: 24.7 us; the launch traced here: 24.5 us
  starting transfers between devices  8.57 us (35%)
  Pallas kernels  7.69 us (31%)
  waiting for transfers between devices  6.26 us (25%)
  between operations  1.38 us (6%)
  other arithmetic  0.63 us (3%)
    ppermute x4, starting transfers between devices, fetched(): return lax.ppermute(value, ('tm', 'chan'), pairs)  8.05 us
    pallas_call x1, Pallas kernels, tile_best(): pl.pallas_call(tile_kernel, out_shape=jax.ShapeDtypeStruct((2, rows), jnp...  6.44 us
    ppermute x4, waiting for transfers between devices, fetched(): return lax.ppermute(value, ('tm', 'chan'), pairs)  4.79 us
    ppermute x2, waiting for transfers between devices, swapped(): return lax.ppermute(value, 'chan', [(0, 1), (1, 0)])  1.47 us
    pallas_call x1, Pallas kernels, project(): pl.pallas_call(functools.partial(project_kernel, chunk), out_shape=pltpu....  1.25 us
    max x1, other arithmetic, per_device(): return jnp.maximum(own, swapped(own))  0.56 us
    ppermute x2, starting transfers between devices, swapped(): return lax.ppermute(value, 'chan', [(0, 1), (1, 0)])  0.52 us
  transfers between devices with their start and end apart: 6, of which 4 were waited for; matrix products, arithmetic and copies ran while one was open for 0% of the time, Pallas kernels for 0%

profile of v8, /device:TPU:0, one launch (start us, length us, event | category | flops | bytes accessed | tf_op | source)
XLA Modules:
  0.0 24.5 jit_solution(12537027039100786523)
XLA Ops:
  0.0 1.3 %project.1 = f32[256,128]{1,0:T(8,128)S(1)} custom-call(bf16[256,512]{1,0:T(8,128)(2,1)} %record.1, bf16[512,128]{1,0:T(8,128)(2,1)} %pca_map.1), custom_call_target="tpu_custom_call" | custom-call | tf_op jit(solution)/shard_map/project/pallas_call | solution.py:158
  1.3 0.5 %collective-permute-start = (f32[256,128]{1,0:T(8,128)S(1)}, f32[256,128]{1,0:T(8,128)S(1)}, u32[]{:S(2)}, u32[]{:S(2)}) collective-permute-start(f32[256,128]{1,0:T(8,128)S(1)} %project.1), channel_id=1, source_target_pairs={{0,1},{1,0},{2,3},{3,2},{4,5},{5,4},{6,7},{7,6},{8,9},{9,8},{10,11... | collective-permute-start | bytes 393224 | tf_op jit(solution)/shard_map/ppermute | solution.py:181
  2.4 0.3 %collective-permute-done = f32[256,128]{1,0:T(8,128)S(1)} collective-permute-done((f32[256,128]{1,0:T(8,128)S(1)}, f32[256,128]{1,0:T(8,128)S(1)}, u32[]{:S(2)}, u32[]{:S(2)}) %collective-permute-start) | collective-permute-done | bytes 131104 | tf_op jit(solution)/shard_map/ppermute | solution.py:181
  2.8 2.9 %collective-permute-start.1 = (bf16[272,128]{1,0:T(8,128)(2,1)S(1)}, bf16[272,128]{1,0:T(8,128)(2,1)S(1)}, u32[]{:S(2)}, u32[]{:S(2)}) collective-permute-start(bf16[272,128]{1,0:T(8,128)(2,1)S(1)} %concatenate.6.c_head), channel_id=1, source_target_pairs={{14,0},{9,1},{0,2},{11,3},{2,4},{13,5},{4,6},{15,7},{6,8},{1,9},{8... | collective-permute-start | bytes 208904 | tf_op jit(solution)/shard_map/ppermute | solution.py:177
  5.7 2.9 %collective-permute-start.2 = (bf16[256,128]{1,0:T(8,128)(2,1)S(1)}, bf16[256,128]{1,0:T(8,128)(2,1)S(1)}, u32[]{:S(2)}, u32[]{:S(2)}) collective-permute-start(bf16[256,128]{1,0:T(8,128)(2,1)S(1)} %add_convert_fusion), channel_id=1, source_target_pairs={{2,0},{11,1},{4,2},{13,3},{6,4},{15,5},{8,6},{1,7},{10,8},{3,9},{1... | collective-permute-start | bytes 196616 | tf_op jit(solution)/shard_map/ppermute | solution.py:177
  8.6 2.2 %collective-permute-start.3 = (bf16[256,128]{1,0:T(8,128)(2,1)S(1)}, bf16[256,128]{1,0:T(8,128)(2,1)S(1)}, u32[]{:S(2)}, u32[]{:S(2)}) collective-permute-start(bf16[256,128]{1,0:T(8,128)(2,1)S(1)} %add_convert_fusion), channel_id=1, source_target_pairs={{1,0},{2,1},{7,2},{4,3},{5,4},{6,5},{11,6},{8,7},{9,8},{10,9},{15,... | collective-permute-start | bytes 196616 | tf_op jit(solution)/shard_map/ppermute | solution.py:177
  11.4 0.0 collective-permute-done.2
  11.5 1.2 %collective-permute-done.3 = bf16[256,128]{1,0:T(8,128)(2,1)S(1)} collective-permute-done((bf16[256,128]{1,0:T(8,128)(2,1)S(1)}, bf16[256,128]{1,0:T(8,128)(2,1)S(1)}, u32[]{:S(2)}, u32[]{:S(2)}) %collective-permute-start.3) | collective-permute-done | bytes 65568 | tf_op jit(solution)/shard_map/ppermute | solution.py:177
  12.7 0.0 collective-permute-done.1
  12.8 6.4 %tile_best.1 = f32[2,256]{1,0:T(2,128)S(1)} custom-call(s32[8,128]{1,0:T(8,128)S(1)} %broadcast_in_dim.7.zone, bf16[272,128]{1,0:T(8,128)(2,1)S(1)} %pad_select_fusion.r_head, bf16[256,128]{1,0:T(8,128)(2,1)S(1)} %get-tuple-element.12.r_tail, bf16[272,128]{1,0:T(8,128)(2,1)S(1)} %concatenate.6.c_head, bf16[256,128]{1,0:T(8,128)(2,1)S(1)} %get-tuple-element.11.c_tail), custom_call_target="tpu_custom_call" | custom-call | tf_op jit(solution)/shard_map/tile_best/pallas_call | solution.py:122
  19.2 0.1 collective-permute-start.4
  19.3 3.5 %collective-permute-done.4 = f32[256]{0:T(256)S(1)} collective-permute-done((f32[256]{0:T(256)S(1)}, f32[256]{0:T(256)S(1)}, u32[]{:S(2)}, u32[]{:S(2)}) %collective-permute-start.4) | collective-permute-done | bytes 1056 | tf_op jit(solution)/shard_map/ppermute | solution.py:177
  22.8 0.0 collective-permute-start.5
  22.8 1.1 %collective-permute-done.5 = f32[256]{0:T(256)S(1)} collective-permute-done((f32[256]{0:T(256)S(1)}, f32[256]{0:T(256)S(1)}, u32[]{:S(2)}, u32[]{:S(2)}) %collective-permute-start.5) | collective-permute-done | bytes 1056 | tf_op jit(solution)/shard_map/ppermute | solution.py:181
  24.0 0.6 %max.7 = f32[256]{0:T(256)} maximum(f32[256]{0:T(256)S(1)} %maximum_select_fusion, f32[256]{0:T(256)S(1)} %collective-permute-done.5) | non-fusion elementwise | flops 256 | bytes 3072 | tf_op jit(solution)/shard_map/max | solution.py:214
  (7 shorter events, 0.1 us)
Async XLA Ops:
  1.3 1.5 %collective-permute-start = (f32[256,128]{1,0:T(8,128)S(1)}, f32[256,128]{1,0:T(8,128)S(1)}, u32[]{:S(2)}, u32[]{:S(2)}) collective-permute-start(f32[256,128]{1,0:T(8,128)S(1)} %project.1), channel_id=1, source_target_pairs={{0,1},{1,0},{2,3},{3,2},{4,5},{5,4},{6,7},{7,6},{8,9},{9,8},{10,11... | collective-permute-start | bytes 393224 | tf_op jit(solution)/shard_map/ppermute | solution.py:181
  2.8 9.9 %collective-permute-start.1 = (bf16[272,128]{1,0:T(8,128)(2,1)S(1)}, bf16[272,128]{1,0:T(8,128)(2,1)S(1)}, u32[]{:S(2)}, u32[]{:S(2)}) collective-permute-start(bf16[272,128]{1,0:T(8,128)(2,1)S(1)} %concatenate.6.c_head), channel_id=1, source_target_pairs={{14,0},{9,1},{0,2},{11,3},{2,4},{13,5},{4,6},{15,7},{6,8},{1,9},{8... | collective-permute-start | bytes 208904 | tf_op jit(solution)/shard_map/ppermute | solution.py:177
  5.7 5.7 %collective-permute-start.2 = (bf16[256,128]{1,0:T(8,128)(2,1)S(1)}, bf16[256,128]{1,0:T(8,128)(2,1)S(1)}, u32[]{:S(2)}, u32[]{:S(2)}) collective-permute-start(bf16[256,128]{1,0:T(8,128)(2,1)S(1)} %add_convert_fusion), channel_id=1, source_target_pairs={{2,0},{11,1},{4,2},{13,3},{6,4},{15,5},{8,6},{1,7},{10,8},{3,9},{1... | collective-permute-start | bytes 196616 | tf_op jit(solution)/shard_map/ppermute | solution.py:177
  8.6 4.1 %collective-permute-start.3 = (bf16[256,128]{1,0:T(8,128)(2,1)S(1)}, bf16[256,128]{1,0:T(8,128)(2,1)S(1)}, u32[]{:S(2)}, u32[]{:S(2)}) collective-permute-start(bf16[256,128]{1,0:T(8,128)(2,1)S(1)} %add_convert_fusion), channel_id=1, source_target_pairs={{1,0},{2,1},{7,2},{4,3},{5,4},{6,5},{11,6},{8,7},{9,8},{10,9},{15,... | collective-permute-start | bytes 196616 | tf_op jit(solution)/shard_map/ppermute | solution.py:177
  19.2 3.6 %collective-permute-start.4 = (f32[256]{0:T(256)S(1)}, f32[256]{0:T(256)S(1)}, u32[]{:S(2)}, u32[]{:S(2)}) collective-permute-start(f32[256]{0:T(256)S(1)} %bitcast.6), channel_id=1, source_target_pairs={{2,0},{0,1},{4,2},{1,3},{6,4},{3,5},{8,6},{5,7},{10,8},{13,9},{12,... | collective-permute-start | bytes 3080 | tf_op jit(solution)/shard_map/ppermute | solution.py:177
  22.8 1.1 %collective-permute-start.5 = (f32[256]{0:T(256)S(1)}, f32[256]{0:T(256)S(1)}, u32[]{:S(2)}, u32[]{:S(2)}) collective-permute-start(f32[256]{0:T(256)S(1)} %maximum_select_fusion), channel_id=1, source_target_pairs={{0,1},{1,0},{2,3},{3,2},{4,5},{5,4},{6,7},{7,6},{8,9},{9,8},{10,11... | collective-permute-start | bytes 3080 | tf_op jit(solution)/shard_map/ppermute | solution.py:181

commit v9 on v8

--- a/solution.py
+++ b/solution.py
@@ -8,7 +8,7 @@
 from jax.sharding import PartitionSpec as P
 
 M = 256
-SHIFTS = 64
+SHIFTS = 128
 BLOCK = 64
 NEG = -1e30
 UNITS = 2
@@ -51,7 +51,7 @@
             mean = sums[:, :depth] / M
             spread = squares / M - mean * mean
             center[side] = mean
-            inverse[side] = (1.0 / (jnp.sqrt(spread + 1e-05) * scale))
+            inverse[side] = (lax.rsqrt(spread + 1e-05) * (1.0 / scale))
 
     in_unit(scoped, (rows, 2 * depth), (0, 1, 0, 1))
 
@@ -194,15 +194,18 @@
     last = cycle - 1
     edge = (core == 1) & (lax.axis_index("tm") == last)
     first = [(((turn - 1) % cycle, 0), ((turn + half) % cycle, 1)) for turn in turns]
-    second = [((turn + 1, 0), ((turn + half + 1) % cycle, 1)) for turn in turns[:-1]] + [((half, 1), (0, 0))]
-    third = [((turn, 1), (turn + 1, 0)) for turn in turns[:-1]] + [((0, 0), (1, 1))]
+    second = [(((turn + 1) % cycle, 0), ((turn + half + 1) % cycle, 1)) for turn in turns]
+    second[half - 1], second[last] = ((half, 0), (half, 1)), ((0, 0), (0, 1))
+    third = [((turn, 1), ((turn + 1) % cycle, 0)) for turn in turns]
     for turn in range(1, last, 2):
         third[turn] = ((turn + 2, 1), third[turn][1])
+    third[half - 1], third[last] = (third[half - 1][0], (0, 0)), ((half, 0), (1, 1))
     r_head, second, third = [fetched(noted, first), fetched(proj, second), fetched(proj, third)]
     r_head, second, third = lax.optimization_barrier((r_head, second, third))
     r_head = jnp.where(edge, jnp.concatenate([second, note], axis=0), r_head)
-    r_tail = jnp.where(core == 0, proj, jnp.where(edge, third, second))
-    c_tail = jnp.where((core == 1) ^ (lax.axis_index("tm") == last), third, second)
+    turned = (core == 1) & (lax.axis_index("tm") % half == half - 1)
+    r_tail = jnp.where(core == 0, proj, jnp.where(turned, third, second))
+    c_tail = jnp.where((core == 1) & ~turned, third, second)
     zone = jnp.broadcast_to(exclusion[:, None], (8, proj.shape[1]))
     best = tile_best(zone, r_head, r_tail, noted, c_tail)
     beyond = [(turn - 1, 1) for turn in turns]

time: 24.7 us -> 24.3 us (0.984)
  the two profiles are of different devices: /device:TPU:0 before, /device:TPU:15 now
where the time goes in v9:
time: 24.3 us; the launch traced here: 24.1 us
  starting transfers between devices  7.49 us (31%)
  Pallas kernels  7.48 us (31%)
  waiting for transfers between devices  7.17 us (30%)
  between operations  1.36 us (6%)
  other arithmetic  0.63 us (3%)
    pallas_call x1, Pallas kernels, tile_best(): pl.pallas_call(tile_kernel, out_shape=jax.ShapeDtypeStruct((2, rows), jnp...  6.23 us
    ppermute x4, waiting for transfers between devices, fetched(): return lax.ppermute(value, ('tm', 'chan'), pairs)  6.02 us
    ppermute x4, starting transfers between devices, fetched(): return lax.ppermute(value, ('tm', 'chan'), pairs)  4.02 us
    ppermute x2, starting transfers between devices, swapped(): return lax.ppermute(value, 'chan', [(0, 1), (1, 0)])  3.47 us
    pallas_call x1, Pallas kernels, project(): pl.pallas_call(functools.partial(project_kernel, chunk), out_shape=pltpu....  1.25 us
    ppermute x2, waiting for transfers between devices, swapped(): return lax.ppermute(value, 'chan', [(0, 1), (1, 0)])  1.15 us
    max x1, other arithmetic, per_device(): return jnp.maximum(own, swapped(own))  0.56 us
  transfers between devices with their start and end apart: 6, of which 5 were waited for; matrix products, arithmetic and copies ran while one was open for 0% of the time, Pallas kernels for 0%

profile of v9, /device:TPU:15, one launch (start us, length us, event | category | flops | bytes accessed | tf_op | source)
XLA Modules:
  0.0 24.1 jit_solution(16195277454578515880)
XLA Ops:
  0.0 1.3 %project.1 = f32[256,128]{1,0:T(8,128)S(1)} custom-call(bf16[256,512]{1,0:T(8,128)(2,1)} %record.1, bf16[512,128]{1,0:T(8,128)(2,1)} %pca_map.1), custom_call_target="tpu_custom_call" | custom-call | tf_op jit(solution)/shard_map/project/pallas_call | solution.py:158
  1.3 0.7 %collective-permute-start = (f32[256,128]{1,0:T(8,128)S(1)}, f32[256,128]{1,0:T(8,128)S(1)}, u32[]{:S(2)}, u32[]{:S(2)}) collective-permute-start(f32[256,128]{1,0:T(8,128)S(1)} %project.1), channel_id=1, source_target_pairs={{0,1},{1,0},{2,3},{3,2},{4,5},{5,4},{6,7},{7,6},{8,9},{9,8},{10,11... | collective-permute-start | bytes 393224 | tf_op jit(solution)/shard_map/ppermute | solution.py:181
  2.7 0.3 %collective-permute-done = f32[256,128]{1,0:T(8,128)S(1)} collective-permute-done((f32[256,128]{1,0:T(8,128)S(1)}, f32[256,128]{1,0:T(8,128)S(1)}, u32[]{:S(2)}, u32[]{:S(2)}) %collective-permute-start) | collective-permute-done | bytes 131104 | tf_op jit(solution)/shard_map/ppermute | solution.py:181
  3.0 2.4 %collective-permute-start.1 = (bf16[272,128]{1,0:T(8,128)(2,1)S(1)}, bf16[272,128]{1,0:T(8,128)(2,1)S(1)}, u32[]{:S(2)}, u32[]{:S(2)}) collective-permute-start(bf16[272,128]{1,0:T(8,128)(2,1)S(1)} %concatenate.6.c_head), channel_id=1, source_target_pairs={{14,0},{9,1},{0,2},{11,3},{2,4},{13,5},{4,6},{15,7},{6,8},{1,9},{8... | collective-permute-start | bytes 208904 | tf_op jit(solution)/shard_map/ppermute | solution.py:177
  5.4 0.0 collective-permute-start.2
  5.4 0.1 collective-permute-start.3
  6.2 5.0 %collective-permute-done.2 = bf16[256,128]{1,0:T(8,128)(2,1)S(1)} collective-permute-done((bf16[256,128]{1,0:T(8,128)(2,1)S(1)}, bf16[256,128]{1,0:T(8,128)(2,1)S(1)}, u32[]{:S(2)}, u32[]{:S(2)}) %collective-permute-start.2) | collective-permute-done | bytes 65568 | tf_op jit(solution)/shard_map/ppermute | solution.py:177
  11.2 0.1 collective-permute-done.3
  11.2 0.0 collective-permute-done.1
  11.3 6.2 %tile_best.1 = f32[2,256]{1,0:T(2,128)S(1)} custom-call(s32[8,128]{1,0:T(8,128)S(1)} %broadcast_in_dim.7.zone, bf16[272,128]{1,0:T(8,128)(2,1)S(1)} %pad_select_fusion.r_head, bf16[256,128]{1,0:T(8,128)(2,1)S(1)} %get-tuple-element.12.r_tail, bf16[272,128]{1,0:T(8,128)(2,1)S(1)} %concatenate.6.c_head, bf16[256,128]{1,0:T(8,128)(2,1)S(1)} %get-tuple-element.11.c_tail), custom_call_target="tpu_custom_call" | custom-call | tf_op jit(solution)/shard_map/tile_best/pallas_call | solution.py:122
  17.5 1.5 %collective-permute-start.4 = (f32[256]{0:T(256)S(1)}, f32[256]{0:T(256)S(1)}, u32[]{:S(2)}, u32[]{:S(2)}) collective-permute-start(f32[256]{0:T(256)S(1)} %bitcast.6), channel_id=1, source_target_pairs={{2,0},{0,1},{4,2},{1,3},{6,4},{3,5},{8,6},{5,7},{10,8},{13,9},{12,... | collective-permute-start | bytes 3080 | tf_op jit(solution)/shard_map/ppermute | solution.py:177
  19.1 1.0 %collective-permute-done.4 = f32[256]{0:T(256)S(1)} collective-permute-done((f32[256]{0:T(256)S(1)}, f32[256]{0:T(256)S(1)}, u32[]{:S(2)}, u32[]{:S(2)}) %collective-permute-start.4) | collective-permute-done | bytes 1056 | tf_op jit(solution)/shard_map/ppermute | solution.py:177
  20.0 2.7 %collective-permute-start.5 = (f32[256]{0:T(256)S(1)}, f32[256]{0:T(256)S(1)}, u32[]{:S(2)}, u32[]{:S(2)}) collective-permute-start(f32[256]{0:T(256)S(1)} %maximum_select_fusion), channel_id=1, source_target_pairs={{0,1},{1,0},{2,3},{3,2},{4,5},{5,4},{6,7},{7,6},{8,9},{9,8},{10,11... | collective-permute-start | bytes 3080 | tf_op jit(solution)/shard_map/ppermute | solution.py:181
  22.8 0.8 %collective-permute-done.5 = f32[256]{0:T(256)S(1)} collective-permute-done((f32[256]{0:T(256)S(1)}, f32[256]{0:T(256)S(1)}, u32[]{:S(2)}, u32[]{:S(2)}) %collective-permute-start.5) | collective-permute-done | bytes 1056 | tf_op jit(solution)/shard_map/ppermute | solution.py:181
  23.6 0.6 %max.7 = f32[256]{0:T(256)} maximum(f32[256]{0:T(256)S(1)} %maximum_select_fusion, f32[256]{0:T(256)S(1)} %collective-permute-done.5) | non-fusion elementwise | flops 256 | bytes 3072 | tf_op jit(solution)/shard_map/max | solution.py:217
  (7 shorter events, 0.1 us)
Async XLA Ops:
  1.3 1.7 %collective-permute-start = (f32[256,128]{1,0:T(8,128)S(1)}, f32[256,128]{1,0:T(8,128)S(1)}, u32[]{:S(2)}, u32[]{:S(2)}) collective-permute-start(f32[256,128]{1,0:T(8,128)S(1)} %project.1), channel_id=1, source_target_pairs={{0,1},{1,0},{2,3},{3,2},{4,5},{5,4},{6,7},{7,6},{8,9},{9,8},{10,11... | collective-permute-start | bytes 393224 | tf_op jit(solution)/shard_map/ppermute | solution.py:181
  3.0 8.2 %collective-permute-start.1 = (bf16[272,128]{1,0:T(8,128)(2,1)S(1)}, bf16[272,128]{1,0:T(8,128)(2,1)S(1)}, u32[]{:S(2)}, u32[]{:S(2)}) collective-permute-start(bf16[272,128]{1,0:T(8,128)(2,1)S(1)} %concatenate.6.c_head), channel_id=1, source_target_pairs={{14,0},{9,1},{0,2},{11,3},{2,4},{13,5},{4,6},{15,7},{6,8},{1,9},{8... | collective-permute-start | bytes 208904 | tf_op jit(solution)/shard_map/ppermute | solution.py:177
  5.4 5.8 %collective-permute-start.2 = (bf16[256,128]{1,0:T(8,128)(2,1)S(1)}, bf16[256,128]{1,0:T(8,128)(2,1)S(1)}, u32[]{:S(2)}, u32[]{:S(2)}) collective-permute-start(bf16[256,128]{1,0:T(8,128)(2,1)S(1)} %add_convert_fusion), channel_id=1, source_target_pairs={{2,0},{11,1},{4,2},{13,3},{6,4},{15,5},{8,6},{9,7},{10,8},{3,9},{1... | collective-permute-start | bytes 196616 | tf_op jit(solution)/shard_map/ppermute | solution.py:177
  5.4 5.8 %collective-permute-start.3 = (bf16[256,128]{1,0:T(8,128)(2,1)S(1)}, bf16[256,128]{1,0:T(8,128)(2,1)S(1)}, u32[]{:S(2)}, u32[]{:S(2)}) collective-permute-start(bf16[256,128]{1,0:T(8,128)(2,1)S(1)} %add_convert_fusion), channel_id=1, source_target_pairs={{1,0},{2,1},{7,2},{4,3},{5,4},{6,5},{11,6},{0,7},{9,8},{10,9},{15,... | collective-permute-start | bytes 196616 | tf_op jit(solution)/shard_map/ppermute | solution.py:177
  17.5 2.5 %collective-permute-start.4 = (f32[256]{0:T(256)S(1)}, f32[256]{0:T(256)S(1)}, u32[]{:S(2)}, u32[]{:S(2)}) collective-permute-start(f32[256]{0:T(256)S(1)} %bitcast.6), channel_id=1, source_target_pairs={{2,0},{0,1},{4,2},{1,3},{6,4},{3,5},{8,6},{5,7},{10,8},{13,9},{12,... | collective-permute-start | bytes 3080 | tf_op jit(solution)/shard_map/ppermute | solution.py:177
  20.0 3.6 %collective-permute-start.5 = (f32[256]{0:T(256)S(1)}, f32[256]{0:T(256)S(1)}, u32[]{:S(2)}, u32[]{:S(2)}) collective-permute-start(f32[256]{0:T(256)S(1)} %maximum_select_fusion), channel_id=1, source_target_pairs={{0,1},{1,0},{2,3},{3,2},{4,5},{5,4},{6,7},{7,6},{8,9},{9,8},{10,11... | collective-permute-start | bytes 3080 | tf_op jit(solution)/shard_map/ppermute | solution.py:181

commit v10 on v9

--- a/solution.py
+++ b/solution.py
@@ -195,7 +195,7 @@
     edge = (core == 1) & (lax.axis_index("tm") == last)
     first = [(((turn - 1) % cycle, 0), ((turn + half) % cycle, 1)) for turn in turns]
     second = [(((turn + 1) % cycle, 0), ((turn + half + 1) % cycle, 1)) for turn in turns]
-    second[half - 1], second[last] = ((half, 0), (half, 1)), ((0, 0), (0, 1))
+    second[half - 1], second[last] = ((half, 1), (half, 0)), ((0, 0), (0, 1))
     third = [((turn, 1), ((turn + 1) % cycle, 0)) for turn in turns]
     for turn in range(1, last, 2):
         third[turn] = ((turn + 2, 1), third[turn][1])

time: 24.3 us -> 23.2 us (0.955)
  the two profiles are of different devices: /device:TPU:15 before, /device:TPU:0 now
where the time goes in v10:
time: 23.2 us; the launch traced here: 23 us
  starting transfers between devices  7.82 us (34%)
  Pallas kernels  7.48 us (32%)
  waiting for transfers between devices  5.72 us (25%)
  between operations  1.36 us (6%)
  other arithmetic  0.63 us (3%)
    ppermute x4, starting transfers between devices, fetched(): return lax.ppermute(value, ('tm', 'chan'), pairs)  7.3 us
    pallas_call x1, Pallas kernels, tile_best(): pl.pallas_call(tile_kernel, out_shape=jax.ShapeDtypeStruct((2, rows), jnp...  6.23 us
    ppermute x4, waiting for transfers between devices, fetched(): return lax.ppermute(value, ('tm', 'chan'), pairs)  4.25 us
    ppermute x2, waiting for transfers between devices, swapped(): return lax.ppermute(value, 'chan', [(0, 1), (1, 0)])  1.47 us
    pallas_call x1, Pallas kernels, project(): pl.pallas_call(functools.partial(project_kernel, chunk), out_shape=pltpu....  1.25 us
    max x1, other arithmetic, per_device(): return jnp.maximum(own, swapped(own))  0.56 us
    ppermute x2, starting transfers between devices, swapped(): return lax.ppermute(value, 'chan', [(0, 1), (1, 0)])  0.52 us
  transfers between devices with their start and end apart: 6, of which 5 were waited for; matrix products, arithmetic and copies ran while one was open for 0% of the time, Pallas kernels for 0%

profile of v10, /device:TPU:0, one launch (start us, length us, event | category | flops | bytes accessed | tf_op | source)
XLA Modules:
  0.0 23.0 jit_solution(13736094150711900818)
XLA Ops:
  0.0 1.3 %project.1 = f32[256,128]{1,0:T(8,128)S(1)} custom-call(bf16[256,512]{1,0:T(8,128)(2,1)} %record.1, bf16[512,128]{1,0:T(8,128)(2,1)} %pca_map.1), custom_call_target="tpu_custom_call" | custom-call | tf_op jit(solution)/shard_map/project/pallas_call | solution.py:158
  1.3 0.5 %collective-permute-start = (f32[256,128]{1,0:T(8,128)S(1)}, f32[256,128]{1,0:T(8,128)S(1)}, u32[]{:S(2)}, u32[]{:S(2)}) collective-permute-start(f32[256,128]{1,0:T(8,128)S(1)} %project.1), channel_id=1, source_target_pairs={{0,1},{1,0},{2,3},{3,2},{4,5},{5,4},{6,7},{7,6},{8,9},{9,8},{10,11... | collective-permute-start | bytes 393224 | tf_op jit(solution)/shard_map/ppermute | solution.py:181
  2.4 0.3 %collective-permute-done = f32[256,128]{1,0:T(8,128)S(1)} collective-permute-done((f32[256,128]{1,0:T(8,128)S(1)}, f32[256,128]{1,0:T(8,128)S(1)}, u32[]{:S(2)}, u32[]{:S(2)}) %collective-permute-start) | collective-permute-done | bytes 131104 | tf_op jit(solution)/shard_map/ppermute | solution.py:181
  2.8 2.9 %collective-permute-start.1 = (bf16[272,128]{1,0:T(8,128)(2,1)S(1)}, bf16[272,128]{1,0:T(8,128)(2,1)S(1)}, u32[]{:S(2)}, u32[]{:S(2)}) collective-permute-start(bf16[272,128]{1,0:T(8,128)(2,1)S(1)} %concatenate.6.c_head), channel_id=1, source_target_pairs={{14,0},{9,1},{0,2},{11,3},{2,4},{13,5},{4,6},{15,7},{6,8},{1,9},{8... | collective-permute-start | bytes 208904 | tf_op jit(solution)/shard_map/ppermute | solution.py:177
  5.7 3.1 %collective-permute-start.2 = (bf16[256,128]{1,0:T(8,128)(2,1)S(1)}, bf16[256,128]{1,0:T(8,128)(2,1)S(1)}, u32[]{:S(2)}, u32[]{:S(2)}) collective-permute-start(bf16[256,128]{1,0:T(8,128)(2,1)S(1)} %add_convert_fusion), channel_id=1, source_target_pairs={{2,0},{11,1},{4,2},{13,3},{6,4},{15,5},{9,6},{8,7},{10,8},{3,9},{1... | collective-permute-start | bytes 196616 | tf_op jit(solution)/shard_map/ppermute | solution.py:177
  8.8 0.0 collective-permute-start.3
  9.5 1.3 %collective-permute-done.2 = bf16[256,128]{1,0:T(8,128)(2,1)S(1)} collective-permute-done((bf16[256,128]{1,0:T(8,128)(2,1)S(1)}, bf16[256,128]{1,0:T(8,128)(2,1)S(1)}, u32[]{:S(2)}, u32[]{:S(2)}) %collective-permute-start.2) | collective-permute-done | bytes 65568 | tf_op jit(solution)/shard_map/ppermute | solution.py:177
  10.7 0.6 %collective-permute-done.3 = bf16[256,128]{1,0:T(8,128)(2,1)S(1)} collective-permute-done((bf16[256,128]{1,0:T(8,128)(2,1)S(1)}, bf16[256,128]{1,0:T(8,128)(2,1)S(1)}, u32[]{:S(2)}, u32[]{:S(2)}) %collective-permute-start.3) | collective-permute-done | bytes 65568 | tf_op jit(solution)/shard_map/ppermute | solution.py:177
  11.4 0.0 collective-permute-done.1
  11.4 6.2 %tile_best.1 = f32[2,256]{1,0:T(2,128)S(1)} custom-call(s32[8,128]{1,0:T(8,128)S(1)} %broadcast_in_dim.7.zone, bf16[272,128]{1,0:T(8,128)(2,1)S(1)} %pad_select_fusion.r_head, bf16[256,128]{1,0:T(8,128)(2,1)S(1)} %get-tuple-element.12.r_tail, bf16[272,128]{1,0:T(8,128)(2,1)S(1)} %concatenate.6.c_head, bf16[256,128]{1,0:T(8,128)(2,1)S(1)} %get-tuple-element.11.c_tail), custom_call_target="tpu_custom_call" | custom-call | tf_op jit(solution)/shard_map/tile_best/pallas_call | solution.py:122
  17.7 1.3 %collective-permute-start.4 = (f32[256]{0:T(256)S(1)}, f32[256]{0:T(256)S(1)}, u32[]{:S(2)}, u32[]{:S(2)}) collective-permute-start(f32[256]{0:T(256)S(1)} %bitcast.6), channel_id=1, source_target_pairs={{2,0},{0,1},{4,2},{1,3},{6,4},{3,5},{8,6},{5,7},{10,8},{13,9},{12,... | collective-permute-start | bytes 3080 | tf_op jit(solution)/shard_map/ppermute | solution.py:177
  18.9 2.4 %collective-permute-done.4 = f32[256]{0:T(256)S(1)} collective-permute-done((f32[256]{0:T(256)S(1)}, f32[256]{0:T(256)S(1)}, u32[]{:S(2)}, u32[]{:S(2)}) %collective-permute-start.4) | collective-permute-done | bytes 1056 | tf_op jit(solution)/shard_map/ppermute | solution.py:177
  21.3 0.0 collective-permute-start.5
  21.3 1.1 %collective-permute-done.5 = f32[256]{0:T(256)S(1)} collective-permute-done((f32[256]{0:T(256)S(1)}, f32[256]{0:T(256)S(1)}, u32[]{:S(2)}, u32[]{:S(2)}) %collective-permute-start.5) | collective-permute-done | bytes 1056 | tf_op jit(solution)/shard_map/ppermute | solution.py:181
  22.4 0.6 %max.7 = f32[256]{0:T(256)} maximum(f32[256]{0:T(256)S(1)} %maximum_select_fusion, f32[256]{0:T(256)S(1)} %collective-permute-done.5) | non-fusion elementwise | flops 256 | bytes 3072 | tf_op jit(solution)/shard_map/max | solution.py:217
  (7 shorter events, 0.1 us)
Async XLA Ops:
  1.3 1.5 %collective-permute-start = (f32[256,128]{1,0:T(8,128)S(1)}, f32[256,128]{1,0:T(8,128)S(1)}, u32[]{:S(2)}, u32[]{:S(2)}) collective-permute-start(f32[256,128]{1,0:T(8,128)S(1)} %project.1), channel_id=1, source_target_pairs={{0,1},{1,0},{2,3},{3,2},{4,5},{5,4},{6,7},{7,6},{8,9},{9,8},{10,11... | collective-permute-start | bytes 393224 | tf_op jit(solution)/shard_map/ppermute | solution.py:181
  2.8 8.6 %collective-permute-start.1 = (bf16[272,128]{1,0:T(8,128)(2,1)S(1)}, bf16[272,128]{1,0:T(8,128)(2,1)S(1)}, u32[]{:S(2)}, u32[]{:S(2)}) collective-permute-start(bf16[272,128]{1,0:T(8,128)(2,1)S(1)} %concatenate.6.c_head), channel_id=1, source_target_pairs={{14,0},{9,1},{0,2},{11,3},{2,4},{13,5},{4,6},{15,7},{6,8},{1,9},{8... | collective-permute-start | bytes 208904 | tf_op jit(solution)/shard_map/ppermute | solution.py:177
  5.7 5.0 %collective-permute-start.2 = (bf16[256,128]{1,0:T(8,128)(2,1)S(1)}, bf16[256,128]{1,0:T(8,128)(2,1)S(1)}, u32[]{:S(2)}, u32[]{:S(2)}) collective-permute-start(bf16[256,128]{1,0:T(8,128)(2,1)S(1)} %add_convert_fusion), channel_id=1, source_target_pairs={{2,0},{11,1},{4,2},{13,3},{6,4},{15,5},{9,6},{8,7},{10,8},{3,9},{1... | collective-permute-start | bytes 196616 | tf_op jit(solution)/shard_map/ppermute | solution.py:177
  8.8 2.5 %collective-permute-start.3 = (bf16[256,128]{1,0:T(8,128)(2,1)S(1)}, bf16[256,128]{1,0:T(8,128)(2,1)S(1)}, u32[]{:S(2)}, u32[]{:S(2)}) collective-permute-start(bf16[256,128]{1,0:T(8,128)(2,1)S(1)} %add_convert_fusion), channel_id=1, source_target_pairs={{1,0},{2,1},{7,2},{4,3},{5,4},{6,5},{11,6},{0,7},{9,8},{10,9},{15,... | collective-permute-start | bytes 196616 | tf_op jit(solution)/shard_map/ppermute | solution.py:177
  17.7 3.6 %collective-permute-start.4 = (f32[256]{0:T(256)S(1)}, f32[256]{0:T(256)S(1)}, u32[]{:S(2)}, u32[]{:S(2)}) collective-permute-start(f32[256]{0:T(256)S(1)} %bitcast.6), channel_id=1, source_target_pairs={{2,0},{0,1},{4,2},{1,3},{6,4},{3,5},{8,6},{5,7},{10,8},{13,9},{12,... | collective-permute-start | bytes 3080 | tf_op jit(solution)/shard_map/ppermute | solution.py:177
  21.3 1.1 %collective-permute-start.5 = (f32[256]{0:T(256)S(1)}, f32[256]{0:T(256)S(1)}, u32[]{:S(2)}, u32[]{:S(2)}) collective-permute-start(f32[256]{0:T(256)S(1)} %maximum_select_fusion), channel_id=1, source_target_pairs={{0,1},{1,0},{2,3},{3,2},{4,5},{5,4},{6,7},{7,6},{8,9},{9,8},{10,11... | collective-permute-start | bytes 3080 | tf_op jit(solution)/shard_map/ppermute | solution.py:181
